TPU v7x, 128 devices: a whole 4x4x4 slice. The times are simulated.
128 devices in a mesh: segment: 4 (over y_lo, core), slab: 32 (over x, y_hi, z).
Axes of the slice: x: 4, y: 4 (y_hi: 2, y_lo: 2; y = y_hi * 2 + y_lo), z: 4, core: 2. Of those that a mesh axis runs over, the one named last changes fastest.
Arguments:
- raw_views: bfloat16 [2, 736, 4096], P(None, None, 'slab'), may hold values from -6 to 6
- tap_channel: int32 [736], replicated, may hold values from 0 to 734
- tap_view: int32 [736], replicated, may hold values from 0 to 2
- tap_weight: float32 [736], replicated, may hold values from 0 to 1
- batch_view: int32 [2], replicated, may hold values from 0 to 1151
- footprint: int32 [2, 32, 12], P(None, 'slab'), may hold values from 0 to 31, all different within a row
- plane_weight: bfloat16 [2, 32, 256, 128], P(None, 'slab'), may hold values from -0.5 to 0.5
Outputs:
- image: float32 [32, 256, 4096], P('slab', 'segment')
Inputs may be any that keep to these rules, and one draw needn't show every extreme that they name: Each row of footprint names 12 distinct tiles.
All inputs are finite; a program needn't handle non-finite values.
Results may differ from a plain program's by a relative error of at most 0.0066.
Values may be sent and summed in bfloat16 or wider, within the bound.
No kernel may reach another device: no remote copies, remote signals or barrier semaphores. Data moves between devices by JAX's collectives and lax.ppermute only.
A program may use at most 128 MiB of HBM per device.

v0:
```python
import functools
import math

import jax
import jax.numpy as jnp
import numpy as np
from jax import lax
from jax.experimental import pallas as pl
from jax.experimental.pallas import tpu as pltpu
from jax.sharding import PartitionSpec as P

CH = 736
CHP = 768
ROWS = 64
COLS = 128
PIX = 1024
YR = 4
VPT = 1152
FOOT = 12
TZ = 256
PAY = CH + TZ + 16
STRIP = 128
STRIPS = PIX // STRIP
AXES = ("segment", "slab")
SCALE = CH / PIX
F32 = jnp.float32
BF16 = jnp.bfloat16


def linear(x, y, z, core):
    return ((y % 2) * 2 + core) * 32 + (x % 4) * 8 + (y // 2) * 4 + z % 4


def devices():
    for x in range(4):
        for y in range(4):
            for z in range(4):
                for core in range(2):
                    yield x, y, z, core


def home(slab, batch, core):
    x, y_hi, z = slab // 8, slab // 4 % 2, slab % 4
    return linear(x, batch if y_hi == 0 else 3 - batch, z, core)


def batch_of(y):
    return y % 2 ^ y // 2


def main_pairs():
    return [
        (home(x * 8 + core * 4 + z, batch_of(y), core), linear(x, y, z, core))
        for x, y, z, core in devices()
        if core != y // 2
    ]


def side_pairs(shift):
    pairs = []
    for x, y, z, core in devices():
        slab = x * 8 + core * 4 + z + shift
        if 0 <= slab < 32:
            pairs.append((home(slab, batch_of(y), y // 2), linear(x, y, z, core)))
    return pairs


def torus_pairs(even, odd):
    pairs = []
    for x, y, z, core in devices():
        dx, dz = odd if (x + z) % 2 else even
        pairs.append((linear(x + dx, y, z + dz, core), linear(x, y, z, core)))
    return pairs


A1, B1, C1 = ((2, 0), (0, 2)), ((0, 1), (1, 0)), ((0, -1), (-1, 0))
NEAR = (
    (0, (1, 0), (0, 1)),
    (0, (-1, 0), (0, -1)),
    (1, (0, 1), (1, 0)),
    (1, (0, -1), (-1, 0)),
)
FAR = ((0, (0, 1), (1, 0)), (3, (-1, 0), (0, -1)))


def block_table():
    table = np.zeros((16, 16), np.int32)
    for x in range(4):
        for z in range(4):

            def first(px, pz):
                odd = (px + pz) % 2
                out = [(px, pz)]
                for offsets in (A1, B1, C1):
                    dx, dz = offsets[odd]
                    out.append((px + dx, pz + dz))
                return out

            found = first(x, z)

            def second(px, pz, arrival):
                which, even, odd = NEAR[arrival]
                dx, dz = odd if (px + pz) % 2 else even
                source = first(px + dx, pz + dz)
                return source[:2] if which == 0 else source[2:]

            for arrival in range(4):
                found += second(x, z, arrival)
            for arrival, even, odd in FAR:
                dx, dz = odd if (x + z) % 2 else even
                found += second(x + dx, z + dz, arrival)
            found = [(px % 4, pz % 4) for px, pz in found]
            assert len(set(found)) == 16
            table[x * 4 + z] = [px * 8 + pz for px, pz in found]
    return table


def ramp_matrix():
    distance = np.arange(CH)[:, None] - np.arange(CHP)[None, :]
    odd = distance % 2 != 0
    taps = np.where(odd, -4.0 / (math.pi**2 * np.where(odd, distance, 1) ** 2.0), 0.0)
    taps = np.where(distance == 0, 1.0, taps) * (np.arange(CHP) < CH)
    return jnp.asarray(taps.astype(np.float32).astype(BF16))


def packed(view):
    return jnp.concatenate([view[: CH // 2], view[CH // 2 :]], axis=1)


def unpacked(ref):
    return jnp.concatenate([ref[:, :ROWS], ref[:, ROWS:]], axis=0)


def column(line):
    return jnp.broadcast_to(line.reshape(1, CH), (8, CH)).T[:, :1]


def message_kernel(batch_ref, feet_hbm, raw_hbm, weight_hbm, own_ref, last_ref, first_ref, feet_ref, sem):
    batch = batch_ref[0]
    copies = [
        pltpu.make_async_copy(raw_hbm.at[batch], own_ref.at[pl.ds(0, CH)], sem.at[0]),
        pltpu.make_async_copy(weight_hbm.at[batch, 0], own_ref.at[pl.ds(CH, TZ)], sem.at[1]),
        pltpu.make_async_copy(feet_hbm, feet_ref, sem.at[2]),
    ]
    for copy in copies:
        copy.start()
    for copy in copies:
        copy.wait()
    row = lax.broadcasted_iota(jnp.int32, (16, COLS), 0)
    lane = lax.broadcasted_iota(jnp.int32, (16, COLS), 1)
    feet = jnp.full((16, COLS), -1.0, F32)
    for slot in range(FOOT):
        here = jnp.logical_and(row == 0, lane == slot)
        feet = jnp.where(here, feet_ref[batch, 0, slot].astype(F32), feet)
    own_ref[CH + TZ :, :] = feet.astype(BF16)
    raw = own_ref[:CH, :]
    last_ref[...] = packed(raw[:, ROWS:])
    first_ref[...] = packed(raw[:, :ROWS])


def pair_kernel(one_ref, two_ref, *refs):
    out_ref = refs[-1]
    out_ref[0] = one_ref[...]
    out_ref[1] = two_ref[...]


def filter_kernel(mine_ref, own_ref, other_ref, low_ref, high_ref, channel_ref, view_ref, weight_ref, ramp_ref, out_ref, x_ref, r_ref):
    keep = mine_ref[0] != 0
    both = jnp.where(keep, own_ref[...], other_ref[...])
    raw = both[:CH]
    low = jnp.concatenate([unpacked(low_ref), raw[:, :ROWS]], axis=1)
    high = jnp.concatenate([raw[:, ROWS:], unpacked(high_ref)], axis=1)
    for tap, part in enumerate((low, raw, high)):
        up = jnp.concatenate([part[1:], part[:1]], axis=0)
        x_ref[tap, :CH, :COLS] = part
        x_ref[tap, :CH, COLS:] = up
        x_ref[tap, CH:, :] = jnp.zeros((CHP - CH, 2 * COLS), BF16)
    sources = column(view_ref[...] * CH + channel_ref[...])
    weights = column(weight_ref[...])
    step = CH // 2
    for part in range(2):
        rows = pl.ds(part * step, step)
        total = jnp.zeros((step, 2 * COLS), F32)
        channel = lax.broadcasted_iota(jnp.int32, (step, CHP), 1)
        source = sources[part * step : (part + 1) * step]
        for tap in range(3):
            pick = jnp.where(channel == source - tap * CH, 1.0, 0.0).astype(BF16)
            total += jnp.dot(pick, x_ref[tap], preferred_element_type=F32)
        weight = weights[part * step : (part + 1) * step]
        r_ref[rows, :] = ((1.0 - weight) * total[:, :COLS] + weight * total[:, COLS:]).astype(BF16)
    r_ref[CH:, :] = jnp.zeros((CHP - CH, COLS), BF16)
    out_ref[:CH, :] = jnp.dot(ramp_ref[...], r_ref[...], preferred_element_type=F32).astype(BF16)
    out_ref[CH:, :] = both[CH:]


def weigh(names, tile_ref, g_ref, slot_ref):
    lane = lax.broadcasted_iota(jnp.int32, (16, COLS), 1)
    row = lax.broadcasted_iota(jnp.int32, (16, COLS), 0)
    col = lax.broadcasted_iota(jnp.int32, (TZ, COLS), 1)
    for index, block in enumerate(names):
        feet = block[CH + TZ :, :].astype(F32)
        hit = jnp.logical_and(feet == tile_ref[0].astype(F32), row == 0)
        slot = jnp.sum(jnp.where(hit, lane + 1, 0).astype(F32)).astype(jnp.int32)
        slot_ref[index] = slot

        @pl.when(slot > 0)
        def _():
            weight = block[CH : CH + TZ, :]
            zero = jnp.zeros_like(weight)
            for view in range(2):
                part = jnp.where((col < ROWS) == (view == 0), weight, zero)
                g_ref[index, :, pl.ds(view * TZ, TZ)] = lax.dot_general(
                    block[:CH, :], part, (((1,), (1,)), ((), ())), preferred_element_type=F32
                ).astype(BF16)


def project(base, count, strips, cos_ref, sin_ref, acc_ref, g_ref, slot_ref):
    def one_block(index, carry):
        slot = slot_ref[index]

        @pl.when(slot > 0)
        def _():
            shift = ((slot - 1).astype(F32) - (FOOT - 1) / 2.0) * (PIX / (4.0 * FOOT))
            y_first = shift - (YR / 2.0 - 0.5)
            cos = [cos_ref[2 * (base + index) + view] * SCALE for view in range(2)]
            sin = [sin_ref[2 * (base + index) + view] * SCALE for view in range(2)]
            x_iota = lax.broadcasted_iota(jnp.int32, (STRIP, COLS), 0).astype(F32)
            c_iota = lax.broadcasted_iota(jnp.int32, (STRIP, COLS), 1).astype(F32)
            slope = [x_iota * cos[view] - c_iota for view in range(2)]
            reach = [
                jnp.minimum(0.0, (STRIP - 1) * cos[view]) + jnp.minimum(0.0, (YR - 1) * sin[view]) - 1.5
                for view in range(2)
            ]
            zero, one = jnp.zeros((), BF16), jnp.ones((), BF16)
            for place, strip in enumerate(strips):
                x_first = strip * STRIP - (PIX / 2.0 - 0.5)
                starts, parts = [], []
                for view in range(2):
                    u = (CH - 1) / 2.0 + x_first * cos[view] + y_first * sin[view]
                    low = jnp.clip(u + reach[view], 0.0, float(CH - COLS)).astype(jnp.int32)
                    start = pl.multiple_of(lax.shift_left(lax.shift_right_logical(low, 4), 4), 16)
                    offset = u - start.astype(F32)
                    starts.append(start)
                    rows = []
                    for y in range(YR):
                        away = jnp.abs((slope[view] + (offset + y * sin[view])).astype(BF16))
                        rows.append(jnp.maximum(zero, one - away))
                    parts.append(jnp.concatenate(rows, axis=0))
                mapped = jnp.concatenate(parts, axis=1)
                right = jnp.concatenate(
                    [
                        g_ref[index, pl.ds(starts[view], COLS), pl.ds(view * TZ, TZ)]
                        for view in range(2)
                    ],
                    axis=0,
                )
                rows = pl.ds(place * (YR * STRIP), YR * STRIP)
                acc_ref[rows, :] += jnp.dot(mapped, right, preferred_element_type=F32)

        return carry

    lax.fori_loop(0, count, one_block, 0)


def first_kernel(tile_ref, cos_ref, sin_ref, b0, b1, b2, b3, acc_ref, g_ref, slot_ref):
    weigh([b0, b1, b2, b3], tile_ref, g_ref, slot_ref)
    acc_ref[...] = jnp.zeros_like(acc_ref)
    project(0, 4, range(STRIPS), cos_ref, sin_ref, acc_ref, g_ref, slot_ref)


def middle_kernel(tile_ref, cos_ref, sin_ref, p0, p1, p2, p3, old_ref, acc_ref, g_ref, slot_ref):
    names = [pair.at[i] for pair in (p0, p1, p2, p3) for i in range(2)]
    weigh(names, tile_ref, g_ref, slot_ref)
    acc_ref[...] = old_ref[...]
    project(4, 8, range(STRIPS), cos_ref, sin_ref, acc_ref, g_ref, slot_ref)


def turn(core, acc_ref, send_ref, keep_ref):
    width = PIX // 2

    def one_strip(strip, carry):
        for y in range(YR):
            rows = pl.ds(pl.multiple_of(strip * (YR * STRIP) + y * STRIP, STRIP), STRIP)
            turned = acc_ref[rows, :].T
            cols = pl.ds(pl.multiple_of(strip * STRIP + y * width, STRIP), STRIP)
            keep_ref[:64, cols] = jnp.where(core == 0, turned[:64], turned[64:128])
            keep_ref[64:, cols] = jnp.where(core == 0, turned[128:192], turned[192:])
            send_ref[:64, cols] = jnp.where(core == 0, turned[64:128], turned[:64]).astype(BF16)
            send_ref[64:, cols] = jnp.where(core == 0, turned[192:], turned[128:192]).astype(BF16)
        return carry

    lax.fori_loop(0, STRIPS // 2, one_strip, 0)


def left_kernel(
    tile_ref, cos_ref, sin_ref, p0, p1, old_ref, send_ref, keep_ref, g_ref, slot_ref, acc_ref
):
    names = [pair.at[i] for pair in (p0, p1) for i in range(2)]
    weigh(names, tile_ref, g_ref, slot_ref)
    acc_ref[...] = old_ref[: PIXELS // 2, :]
    project(12, 4, range(STRIPS // 2), cos_ref, sin_ref, acc_ref, g_ref, slot_ref)
    turn(tile_ref[1], acc_ref, send_ref, keep_ref)


def right_kernel(
    tile_ref, cos_ref, sin_ref, slot_ref, g_ref, old_ref, send_ref, keep_ref, acc_ref
):
    acc_ref[...] = old_ref[PIXELS // 2 :, :]
    project(12, 4, range(STRIPS // 2, STRIPS), cos_ref, sin_ref, acc_ref, g_ref, slot_ref)
    turn(tile_ref[1], acc_ref, send_ref, keep_ref)


def half_kernel(chip_ref, keep_ref, got_ref, *refs):
    send_ref, rest_ref = refs[-2:]
    chip = chip_ref[0]
    mine = pl.ds(pl.multiple_of(chip * 64, 64), 64)
    theirs = pl.ds(pl.multiple_of((1 - chip) * 64, 64), 64)
    send_ref[...] = (keep_ref[theirs, :] + got_ref[theirs, :].astype(F32)).astype(BF16)
    rest_ref[...] = keep_ref[mine, :] + got_ref[mine, :].astype(F32)


def sum_kernel(half, rest_ref, got_ref, *refs):
    out_ref, sum_ref, sem = refs[-3:]
    width = PIX // 2
    copies = []
    for y in range(YR):
        cols = pl.ds(y * width, width)
        sum_ref[:, cols] = rest_ref[:, cols] + got_ref[:, cols].astype(F32)
        place = out_ref.at[0, :, pl.ds(y * PIX + half * width, width)]
        copies.append(pltpu.make_async_copy(sum_ref.at[:, cols], place, sem.at[y]))
    for copy in copies:
        copy.start()
    for copy in copies:
        copy.wait()


VMEM = pl.BlockSpec(memory_space=pltpu.VMEM)
SMEM = pl.BlockSpec(memory_space=pltpu.SMEM)
HBM = pl.BlockSpec(memory_space=pltpu.HBM)
LATER = pl.BlockSpec(memory_space=pl.ANY)


def stay(array):
    return pltpu.with_memory_space_constraint(array, pltpu.HBM)


def shape(dims, dtype):
    return jax.ShapeDtypeStruct(dims, dtype)


def cost(flops, moved):
    return pl.CostEstimate(flops=flops, bytes_accessed=moved, transcendentals=0)


LIMIT = 24 * 2**20
BLOCK_FLOPS = 2 * 4096 * 256 * 256 + 2 * CH * COLS * 512
PIXELS = YR * PIX


def shards(raw_views, tap_channel, tap_view, tap_weight, batch_view, footprint, plane_weight):
    segment = lax.axis_index("segment")
    slab = lax.axis_index("slab")
    chip, core = segment // 2, segment % 2
    x_pos, y_hi, z_pos = slab // 8, slab // 4 % 2, slab % 4
    batch = jnp.bitwise_xor(chip, y_hi)

    def call(kernel, out_shape, in_specs, *operands, scratch=(), work=(10**5, 10**6), limit=LIMIT):
        many = isinstance(out_shape, tuple)
        return pl.pallas_call(
            kernel,
            out_shape=out_shape,
            in_specs=in_specs,
            out_specs=tuple(SMEM if o.dtype == jnp.int32 else VMEM for o in out_shape) if many else VMEM,
            scratch_shapes=list(scratch),
            compiler_params=pltpu.CompilerParams(vmem_limit_bytes=limit),
            cost_estimate=cost(*work),
        )(*operands)

    own, last, first = call(
        message_kernel,
        (shape((PAY, COLS), BF16), shape((CH // 2, COLS), BF16), shape((CH // 2, COLS), BF16)),
        [SMEM, HBM, HBM, HBM],
        batch[None],
        stay(footprint),
        stay(raw_views),
        stay(plane_weight),
        scratch=[pltpu.SMEM((2, 1, FOOT), jnp.int32), pltpu.SemaphoreType.DMA((3,))],
    )
    other = lax.ppermute(own, AXES, main_pairs())
    low = lax.ppermute(last, AXES, side_pairs(-1))
    high = lax.ppermute(first, AXES, side_pairs(1))

    payload = call(
        filter_kernel,
        shape((PAY, COLS), BF16),
        [SMEM] + [VMEM] * 8,
        (core == y_hi).astype(jnp.int32)[None],
        own,
        other,
        low,
        high,
        stay(tap_channel),
        stay(tap_view),
        stay(tap_weight),
        stay(ramp_matrix()),
        scratch=[pltpu.VMEM((3, CHP, 2 * COLS), BF16), pltpu.VMEM((CHP, COLS), BF16)],
        work=(4 * 10**9, 4 * 10**6),
    )

    payload, batch_view = lax.optimization_barrier((payload, batch_view))
    got_a = lax.ppermute(payload, AXES, torus_pairs(*A1))
    got_b = lax.ppermute(payload, AXES, torus_pairs(*B1))
    got_c = lax.ppermute(payload, AXES, torus_pairs(*C1))
    blocks = lax.dynamic_index_in_dim(jnp.asarray(block_table()), x_pos * 4 + z_pos, 0, keepdims=False)
    first_view = lax.dynamic_index_in_dim(batch_view, batch, 0, keepdims=False)
    views = jnp.arange(32, dtype=jnp.int32)
    angle = first_view + 2 * (jnp.repeat(blocks, 2) + core * 4) + views % 2
    theta = angle.astype(F32) * (2.0 * math.pi / VPT)
    cos, sin = jnp.cos(theta), jnp.sin(theta)
    tile = jnp.where(jnp.arange(2) == 0, slab, core).astype(jnp.int32)

    two = shape((2, PAY, COLS), BF16)
    pairs = (
        call(pair_kernel, two, [VMEM, VMEM], payload, got_a),
        call(pair_kernel, two, [VMEM, VMEM] + [SMEM] * 3, got_b, got_c, tile, cos, sin),
    )
    near = [lax.ppermute(pairs[which], AXES, torus_pairs(even, odd)) for which, even, odd in NEAR]

    def scratch(count):
        return [pltpu.VMEM((count, CH, 2 * TZ), BF16), pltpu.SMEM((count,), jnp.int32)]

    accumulator = shape((PIXELS, TZ), F32)
    half = (shape((COLS, PIXELS // 2), BF16), shape((COLS, PIXELS // 2), F32))
    half_scratch = [pltpu.VMEM((PIXELS // 2, TZ), F32)]
    total = call(
        first_kernel, accumulator, [SMEM] * 3 + [VMEM] * 4,
        tile, cos, sin, payload, got_a, got_b, got_c,
        scratch=scratch(4), work=(4 * BLOCK_FLOPS, 5 * 10**6),
    )
    *passed, total = lax.optimization_barrier((*(near[arrival] for arrival, _, _ in FAR), total))
    far = [lax.ppermute(part, AXES, torus_pairs(even, odd)) for part, (_, even, odd) in zip(passed, FAR)]
    total = call(
        middle_kernel, accumulator, [SMEM] * 3 + [VMEM] * 5,
        tile, cos, sin, *near, total,
        scratch=scratch(8), work=(8 * BLOCK_FLOPS, 10**7),
    )
    send_left, keep_left, kept, slots = call(
        left_kernel,
        half + (shape((4, CH, 2 * TZ), BF16), shape((4,), jnp.int32)),
        [SMEM] * 3 + [VMEM] * 3,
        tile, cos, sin, *far, total,
        scratch=half_scratch, work=(2 * BLOCK_FLOPS, 9 * 10**6),
    )
    send_right, keep_right = call(
        right_kernel,
        half,
        [SMEM] * 4 + [VMEM] * 2,
        tile, cos, sin, slots, kept, total,
        scratch=half_scratch, work=(2 * BLOCK_FLOPS, 9 * 10**6),
    )

    beside = [(s * 32 + t, (s ^ 1) * 32 + t) for s in range(4) for t in range(32)]
    across = [(s * 32 + t, (s ^ 2) * 32 + t) for s in range(4) for t in range(32)]
    ends, before = [], []
    for send, keep in ((send_left, keep_left), (send_right, keep_right)):
        swapped = lax.ppermute(send, AXES, beside)
        send, rest = call(
            half_kernel,
            (shape((64, PIXELS // 2), BF16), shape((64, PIXELS // 2), F32)),
            [SMEM, VMEM, VMEM] + [LATER] * len(before),
            chip[None], keep, swapped, *before,
        )
        before = [send]
        ends.append((rest, lax.ppermute(send, AXES, across)))
    image = None
    for half, (rest, swapped) in enumerate(ends):
        image = pl.pallas_call(
            functools.partial(sum_kernel, half),
            out_shape=shape((1, 64, PIXELS), F32),
            in_specs=[VMEM, VMEM] + [LATER] * half,
            out_specs=LATER,
            scratch_shapes=[pltpu.VMEM((64, PIXELS // 2), F32), pltpu.SemaphoreType.DMA((YR,))],
            input_output_aliases={2: 0} if half else {},
            compiler_params=pltpu.CompilerParams(vmem_limit_bytes=LIMIT),
            cost_estimate=cost(10**5, 10**6),
        )(rest, swapped, *([image] * half))
    return image


def solution(mesh):
    return jax.shard_map(
        shards,
        mesh=mesh,
        in_specs=(
            P(None, None, "slab"),
            P(),
            P(),
            P(),
            P(),
            P(None, "slab", None),
            P(None, "slab", None, None),
        ),
        out_specs=P("slab", "segment", None),
        check_vma=False,
    )
```

profile of v0, /device:TPU:1, one launch (start us, length us, event | category | flops | bytes accessed | tf_op | source)
XLA Modules:
  0.0 88.7 jit_solution(1654093063633764647)
XLA Ops:
  0.0 1.1 %shard_map.91 = (bf16[1008,128]{1,0:T(8,128)(2,1)S(1)}, bf16[368,128]{1,0:T(8,128)(2,1)S(1)}, bf16[368,128]{1,0:T(8,128)(2,1)S(1)}) custom-call(s32[1]{0:T(128)} %bitcast.2.batch_ref, s32[2,1,12]{2,1,0:T(1,128)} %feet_hbm.1, bf16[2,736,128]{2,1,0:T(8,128)(2,1)} %raw_hbm.1, bf16[2,1,256,128]{3,2,1,0:T(8,128)(2,1)} %weight_hbm.1), custom_call_target="tpu_custom_call" | custom-call | flops 100000 | bytes 1000000 | tf_op jit(solution)/shard_map/pallas_call | solution.py:369
  1.1 1.3 %collective-permute-start = (bf16[1008,128]{1,0:T(8,128)(2,1)S(1)}, bf16[1008,128]{1,0:T(8,128)(2,1)S(1)}, u32[]{:S(2)}, u32[]{:S(2)}) collective-permute-start(bf16[1008,128]{1,0:T(8,128)(2,1)S(1)} %get-tuple-element.23.own_ref), channel_id=1, source_target_pairs={{100,32},{101,33},{102,34},{103,35},{36,96},{37,97},{38,98},{39,99... | collective-permute-start | bytes 774152 | tf_op jit(solution)/shard_map/ppermute | solution.py:389
  2.4 7.4 %collective-permute-start.1 = (bf16[368,128]{1,0:T(8,128)(2,1)S(1)}, bf16[368,128]{1,0:T(8,128)(2,1)S(1)}, u32[]{:S(2)}, u32[]{:S(2)}) collective-permute-start(bf16[368,128]{1,0:T(8,128)(2,1)S(1)} %get-tuple-element.24), channel_id=1, source_target_pairs={{3,32},{0,1},{68,33},{1,2},{69,34},{2,3},{70,35},{67,96},{64,65},{... | collective-permute-start | bytes 282632 | tf_op jit(solution)/shard_map/ppermute | solution.py:390
  9.8 1.3 %collective-permute-start.2 = (bf16[368,128]{1,0:T(8,128)(2,1)S(1)}, bf16[368,128]{1,0:T(8,128)(2,1)S(1)}, u32[]{:S(2)}, u32[]{:S(2)}) collective-permute-start(bf16[368,128]{1,0:T(8,128)(2,1)S(1)} %get-tuple-element.25), channel_id=1, source_target_pairs={{1,0},{69,32},{2,1},{70,33},{3,2},{71,34},{68,3},{8,35},{65,64},{5... | collective-permute-start | bytes 282632 | tf_op jit(solution)/shard_map/ppermute | solution.py:391
  11.1 4.2 %collective-permute-done.1.low_ref = bf16[368,128]{1,0:T(8,128)(2,1)S(1)} collective-permute-done((bf16[368,128]{1,0:T(8,128)(2,1)S(1)}, bf16[368,128]{1,0:T(8,128)(2,1)S(1)}, u32[]{:S(2)}, u32[]{:S(2)}) %collective-permute-start.1) | collective-permute-done | bytes 94240 | tf_op jit(solution)/shard_map/ppermute | solution.py:390
  15.3 2.6 %collective-permute-done.2.high_ref = bf16[368,128]{1,0:T(8,128)(2,1)S(1)} collective-permute-done((bf16[368,128]{1,0:T(8,128)(2,1)S(1)}, bf16[368,128]{1,0:T(8,128)(2,1)S(1)}, u32[]{:S(2)}, u32[]{:S(2)}) %collective-permute-start.2) | collective-permute-done | bytes 94240 | tf_op jit(solution)/shard_map/ppermute | solution.py:391
  17.9 3.4 %shard_map.92.one_ref.b0 = bf16[1008,128]{1,0:T(8,128)(2,1)S(1)} custom-call(s32[1]{0:T(128)} %bitcast.1.mine_ref, bf16[1008,128]{1,0:T(8,128)(2,1)S(1)} %get-tuple-element.23.own_ref, bf16[1008,128]{1,0:T(8,128)(2,1)S(1)} %collective-permute-done.other_ref, bf16[368,128]{1,0:T(8,128)(2,1)S(1)} %collective-permute-done.1.low_ref, ...), custom_call_target="tpu_custom_call" | custom-call | flops 4000000000 | bytes 4000000 | tf_op jit(solution)/shard_map/pallas_call | solution.py:369
  21.3 2.8 %collective-permute-start.3 = (bf16[1008,128]{1,0:T(8,128)(2,1)S(1)}, bf16[1008,128]{1,0:T(8,128)(2,1)S(1)}, u32[]{:S(2)}, u32[]{:S(2)}) collective-permute-start(bf16[1008,128]{1,0:T(8,128)(2,1)S(1)} %shard_map.92.one_ref.b0), channel_id=1, source_target_pairs={{16,0},{48,32},{3,1},{35,33},{18,2},{50,34},{1,3},{33,35},{80,64},... | collective-permute-start | bytes 774152 | tf_op jit(solution)/shard_map/ppermute | solution.py:411
  24.1 3.0 %collective-permute-start.5 = (bf16[1008,128]{1,0:T(8,128)(2,1)S(1)}, bf16[1008,128]{1,0:T(8,128)(2,1)S(1)}, u32[]{:S(2)}, u32[]{:S(2)}) collective-permute-start(bf16[1008,128]{1,0:T(8,128)(2,1)S(1)} %shard_map.92.one_ref.b0), channel_id=1, source_target_pairs={{1,0},{33,32},{9,1},{41,33},{3,2},{35,34},{11,3},{43,35},{65,64},{... | collective-permute-start | bytes 774152 | tf_op jit(solution)/shard_map/ppermute | solution.py:412
  27.8 1.3 %add_bitcast_fusion = s32[16]{0:T(128)S(1)} fusion(s32[16,16]{1,0:T(8,128)} %constant.92.clone, s32[]{:T(128)S(6)} %select_n.51, s32[]{:T(128)S(6)} %mul.24, s32[]{:T(128)} %bitcast.3), kind=kLoop, calls=%fused_computation.4 | loop fusion | flops 48 | bytes 140 | tf_op jit(solution)/shard_map/add | solution.py:417
  29.4 2.8 %collective-permute-done.5.one_ref.b2 = bf16[1008,128]{1,0:T(8,128)(2,1)S(1)} collective-permute-done((bf16[1008,128]{1,0:T(8,128)(2,1)S(1)}, bf16[1008,128]{1,0:T(8,128)(2,1)S(1)}, u32[]{:S(2)}, u32[]{:S(2)}) %collective-permute-start.5) | collective-permute-done | bytes 258080 | tf_op jit(solution)/shard_map/ppermute | solution.py:412
  32.2 2.4 %collective-permute-done.6.two_ref.b3 = bf16[1008,128]{1,0:T(8,128)(2,1)S(1)} collective-permute-done((bf16[1008,128]{1,0:T(8,128)(2,1)S(1)}, bf16[1008,128]{1,0:T(8,128)(2,1)S(1)}, u32[]{:S(2)}, u32[]{:S(2)}) %collective-permute-start.6) | collective-permute-done | bytes 258080 | tf_op jit(solution)/shard_map/ppermute | solution.py:413
  35.2 1.9 %collective-permute-start.7 = (bf16[2,1008,128]{2,1,0:T(8,128)(2,1)S(1)}, bf16[2,1008,128]{2,1,0:T(8,128)(2,1)S(1)}, u32[]{:S(2)}, u32[]{:S(2)}) collective-permute-start(bf16[2,1008,128]{2,1,0:T(8,128)(2,1)S(1)} %shard_map.94), channel_id=1, source_target_pairs={{3,0},{35,32},{25,1},{57,33},{1,2},{33,34},{27,3},{59,35},{67,64},... | collective-permute-start | bytes 1548296 | tf_op jit(solution)/shard_map/ppermute | solution.py:427
  37.1 0.9 %collective-permute-start.4 = (bf16[2,1008,128]{2,1,0:T(8,128)(2,1)S(1)}, bf16[2,1008,128]{2,1,0:T(8,128)(2,1)S(1)}, u32[]{:S(2)}, u32[]{:S(2)}) collective-permute-start(bf16[2,1008,128]{2,1,0:T(8,128)(2,1)S(1)} %shard_map.93), channel_id=1, source_target_pairs={{8,0},{40,32},{2,1},{34,33},{10,2},{42,34},{0,3},{32,35},{72,64},{... | collective-permute-start | bytes 1548296 | tf_op jit(solution)/shard_map/ppermute | solution.py:427
  38.0 2.3 %collective-permute-start.11 = (bf16[2,1008,128]{2,1,0:T(8,128)(2,1)S(1)}, bf16[2,1008,128]{2,1,0:T(8,128)(2,1)S(1)}, u32[]{:S(2)}, u32[]{:S(2)}) collective-permute-start(bf16[2,1008,128]{2,1,0:T(8,128)(2,1)S(1)} %shard_map.94), channel_id=1, source_target_pairs={{1,0},{33,32},{9,1},{41,33},{3,2},{35,34},{11,3},{43,35},{65,64},{... | collective-permute-start | bytes 1548296 | tf_op jit(solution)/shard_map/ppermute | solution.py:427
  40.4 5.9 %shard_map.95.old_ref = f32[4096,256]{1,0:T(8,128)S(1)} custom-call(s32[2]{0:T(128)S(1)} %compare_select_fusion.refs_0_.tile_ref, f32[32]{0:T(128)S(1)} %cos.3.refs_1_.cos_ref, f32[32]{0:T(128)S(1)} %get-tuple-element.41.refs_2_.sin_ref, bf16[1008,128]{1,0:T(8,128)(2,1)S(1)} %shard_map.92.one_ref.b0, ...), custom_call_target="tpu_custom_call" | custom-call | flops 2533359616 | bytes 5000000 | tf_op jit(solution)/shard_map/pallas_call | solution.py:369
  46.3 0.9 %collective-permute-done.7.p3 = bf16[2,1008,128]{2,1,0:T(8,128)(2,1)S(1)} collective-permute-done((bf16[2,1008,128]{2,1,0:T(8,128)(2,1)S(1)}, bf16[2,1008,128]{2,1,0:T(8,128)(2,1)S(1)}, u32[]{:S(2)}, u32[]{:S(2)}) %collective-permute-start.7) | collective-permute-done | bytes 516128 | tf_op jit(solution)/shard_map/ppermute | solution.py:427
  47.3 1.6 %collective-permute-done.4.p0 = bf16[2,1008,128]{2,1,0:T(8,128)(2,1)S(1)} collective-permute-done((bf16[2,1008,128]{2,1,0:T(8,128)(2,1)S(1)}, bf16[2,1008,128]{2,1,0:T(8,128)(2,1)S(1)}, u32[]{:S(2)}, u32[]{:S(2)}) %collective-permute-start.4) | collective-permute-done | bytes 516128 | tf_op jit(solution)/shard_map/ppermute | solution.py:427
  48.9 2.4 %collective-permute-start.8 = (bf16[2,1008,128]{2,1,0:T(8,128)(2,1)S(1)}, bf16[2,1008,128]{2,1,0:T(8,128)(2,1)S(1)}, u32[]{:S(2)}, u32[]{:S(2)}) collective-permute-start(bf16[2,1008,128]{2,1,0:T(8,128)(2,1)S(1)} %collective-permute-done.4.p0), channel_id=1, source_target_pairs={{1,0},{33,32},{9,1},{41,33},{3,2},{35,34},{11,3},{43,35},{65,64},{... | collective-permute-start | bytes 1548296 | tf_op jit(solution)/shard_map/ppermute | solution.py:441
  51.4 1.0 %collective-permute-done.10.p1 = bf16[2,1008,128]{2,1,0:T(8,128)(2,1)S(1)} collective-permute-done((bf16[2,1008,128]{2,1,0:T(8,128)(2,1)S(1)}, bf16[2,1008,128]{2,1,0:T(8,128)(2,1)S(1)}, u32[]{:S(2)}, u32[]{:S(2)}) %collective-permute-start.10) | collective-permute-done | bytes 516128 | tf_op jit(solution)/shard_map/ppermute | solution.py:427
  52.4 3.1 %shard_map.96.old_ref = f32[4096,256]{1,0:T(8,128)S(1)} custom-call(s32[2]{0:T(128)S(1)} %compare_select_fusion.refs_0_.tile_ref, f32[32]{0:T(128)S(1)} %cos.3.refs_1_.cos_ref, f32[32]{0:T(128)S(1)} %get-tuple-element.41.refs_2_.sin_ref, bf16[2,1008,128]{2,1,0:T(8,128)(2,1)S(1)} %collective-permute-done.4.p0, ...), custom_call_target="tpu_custom_call" | custom-call | flops 5066719232 | bytes 10000000 | tf_op jit(solution)/shard_map/pallas_call | solution.py:369
  55.4 6.0 %collective-permute-done.8.p0 = bf16[2,1008,128]{2,1,0:T(8,128)(2,1)S(1)} collective-permute-done((bf16[2,1008,128]{2,1,0:T(8,128)(2,1)S(1)}, bf16[2,1008,128]{2,1,0:T(8,128)(2,1)S(1)}, u32[]{:S(2)}, u32[]{:S(2)}) %collective-permute-start.8) | collective-permute-done | bytes 516128 | tf_op jit(solution)/shard_map/ppermute | solution.py:441
  61.5 1.1 %collective-permute-done.9.p1 = bf16[2,1008,128]{2,1,0:T(8,128)(2,1)S(1)} collective-permute-done((bf16[2,1008,128]{2,1,0:T(8,128)(2,1)S(1)}, bf16[2,1008,128]{2,1,0:T(8,128)(2,1)S(1)}, u32[]{:S(2)}, u32[]{:S(2)}) %collective-permute-start.9) | collective-permute-done | bytes 516128 | tf_op jit(solution)/shard_map/ppermute | solution.py:441
  62.5 2.8 %shard_map.97 = (bf16[128,2048]{1,0:T(8,128)(2,1)S(1)}, f32[128,2048]{1,0:T(8,128)S(1)}, bf16[4,736,512]{2,1,0:T(8,128)(2,1)S(1)}, s32[4]{0:T(128)S(1)}) custom-call(s32[2]{0:T(128)S(1)} %compare_select_fusion.refs_0_.tile_ref, f32[32]{0:T(128)S(1)} %cos.3.refs_1_.cos_ref, f32[32]{0:T(128)S(1)} %get-tuple-element.41.refs_2_.sin_ref, ...), custom_call_target="tpu_custom_call" | custom-call | flops 1266679808 | bytes 9000000 | tf_op jit(solution)/shard_map/pallas_call | solution.py:369
  65.3 6.0 %collective-permute-start.13 = (bf16[128,2048]{1,0:T(8,128)(2,1)S(1)}, bf16[128,2048]{1,0:T(8,128)(2,1)S(1)}, u32[]{:S(2)}, u32[]{:S(2)}) collective-permute-start(bf16[128,2048]{1,0:T(8,128)(2,1)S(1)} %get-tuple-element.36), channel_id=1, source_target_pairs={{0,32},{1,33},{2,34},{3,35},{4,36},{5,37},{6,38},{7,39},{8,40},{9,... | collective-permute-start | bytes 1572872 | tf_op jit(solution)/shard_map/ppermute | solution.py:466
  71.3 1.6 %shard_map.98 = (bf16[128,2048]{1,0:T(8,128)(2,1)S(1)}, f32[128,2048]{1,0:T(8,128)S(1)}) custom-call(s32[2]{0:T(128)S(1)} %compare_select_fusion.refs_0_.tile_ref, f32[32]{0:T(128)S(1)} %cos.3.refs_1_.cos_ref, f32[32]{0:T(128)S(1)} %get-tuple-element.41.refs_2_.sin_ref, s32[4]{0:T(128)S(1)} %get-tuple-element.31.slot_ref, ...), custom_call_target="tpu_custom_call" | custom-call | flops 1266679808 | bytes 9000000 | tf_op jit(solution)/shard_map/pallas_call | solution.py:369
  72.9 1.0 %collective-permute-start.12 = (bf16[128,2048]{1,0:T(8,128)(2,1)S(1)}, bf16[128,2048]{1,0:T(8,128)(2,1)S(1)}, u32[]{:S(2)}, u32[]{:S(2)}) collective-permute-start(bf16[128,2048]{1,0:T(8,128)(2,1)S(1)} %get-tuple-element.34), channel_id=1, source_target_pairs={{0,32},{1,33},{2,34},{3,35},{4,36},{5,37},{6,38},{7,39},{8,40},{9,... | collective-permute-start | bytes 1572872 | tf_op jit(solution)/shard_map/ppermute | solution.py:466
  74.1 1.3 %collective-permute-done.12.got_ref = bf16[128,2048]{1,0:T(8,128)(2,1)S(1)} collective-permute-done((bf16[128,2048]{1,0:T(8,128)(2,1)S(1)}, bf16[128,2048]{1,0:T(8,128)(2,1)S(1)}, u32[]{:S(2)}, u32[]{:S(2)}) %collective-permute-start.12) | collective-permute-done | bytes 524320 | tf_op jit(solution)/shard_map/ppermute | solution.py:466
  75.7 6.3 %collective-permute-done.15.got_ref = bf16[64,2048]{1,0:T(8,128)(2,1)S(1)} collective-permute-done((bf16[64,2048]{1,0:T(8,128)(2,1)S(1)}, bf16[64,2048]{1,0:T(8,128)(2,1)S(1)}, u32[]{:S(2)}, u32[]{:S(2)}) %collective-permute-start.15) | collective-permute-done | bytes 262176 | tf_op jit(solution)/shard_map/ppermute | solution.py:474
  82.0 0.9 shard_map.101.refs_0_
  82.9 4.7 %collective-permute-done.14.got_ref = bf16[64,2048]{1,0:T(8,128)(2,1)S(1)} collective-permute-done((bf16[64,2048]{1,0:T(8,128)(2,1)S(1)}, bf16[64,2048]{1,0:T(8,128)(2,1)S(1)}, u32[]{:S(2)}, u32[]{:S(2)}) %collective-permute-start.14) | collective-permute-done | bytes 262176 | tf_op jit(solution)/shard_map/ppermute | solution.py:474
  87.6 0.9 shard_map.102
  (21 shorter events, 2.1 us)
Async XLA Ops:
  1.1 16.8 %collective-permute-start = (bf16[1008,128]{1,0:T(8,128)(2,1)S(1)}, bf16[1008,128]{1,0:T(8,128)(2,1)S(1)}, u32[]{:S(2)}, u32[]{:S(2)}) collective-permute-start(bf16[1008,128]{1,0:T(8,128)(2,1)S(1)} %get-tuple-element.23.own_ref), channel_id=1, source_target_pairs={{100,32},{101,33},{102,34},{103,35},{36,96},{37,97},{38,98},{39,99... | collective-permute-start | bytes 774152 | tf_op jit(solution)/shard_map/ppermute | solution.py:389
  2.4 12.9 %collective-permute-start.1 = (bf16[368,128]{1,0:T(8,128)(2,1)S(1)}, bf16[368,128]{1,0:T(8,128)(2,1)S(1)}, u32[]{:S(2)}, u32[]{:S(2)}) collective-permute-start(bf16[368,128]{1,0:T(8,128)(2,1)S(1)} %get-tuple-element.24), channel_id=1, source_target_pairs={{3,32},{0,1},{68,33},{1,2},{69,34},{2,3},{70,35},{67,96},{64,65},{... | collective-permute-start | bytes 282632 | tf_op jit(solution)/shard_map/ppermute | solution.py:390
  9.8 8.1 %collective-permute-start.2 = (bf16[368,128]{1,0:T(8,128)(2,1)S(1)}, bf16[368,128]{1,0:T(8,128)(2,1)S(1)}, u32[]{:S(2)}, u32[]{:S(2)}) collective-permute-start(bf16[368,128]{1,0:T(8,128)(2,1)S(1)} %get-tuple-element.25), channel_id=1, source_target_pairs={{1,0},{69,32},{2,1},{70,33},{3,2},{71,34},{68,3},{8,35},{65,64},{5... | collective-permute-start | bytes 282632 | tf_op jit(solution)/shard_map/ppermute | solution.py:391
  17.9 9.3 %copy-start = (s32[2]{0:T(128)S(1)}, s32[2]{0:T(128)}, u32[]{:S(2)}) copy-start(s32[2]{0:T(128)} %param.13) | copy-start | bytes 28
  21.3 15.8 %collective-permute-start.3 = (bf16[1008,128]{1,0:T(8,128)(2,1)S(1)}, bf16[1008,128]{1,0:T(8,128)(2,1)S(1)}, u32[]{:S(2)}, u32[]{:S(2)}) collective-permute-start(bf16[1008,128]{1,0:T(8,128)(2,1)S(1)} %shard_map.92.one_ref.b0), channel_id=1, source_target_pairs={{16,0},{48,32},{3,1},{35,33},{18,2},{50,34},{1,3},{33,35},{80,64},... | collective-permute-start | bytes 774152 | tf_op jit(solution)/shard_map/ppermute | solution.py:411
  24.1 8.1 %collective-permute-start.5 = (bf16[1008,128]{1,0:T(8,128)(2,1)S(1)}, bf16[1008,128]{1,0:T(8,128)(2,1)S(1)}, u32[]{:S(2)}, u32[]{:S(2)}) collective-permute-start(bf16[1008,128]{1,0:T(8,128)(2,1)S(1)} %shard_map.92.one_ref.b0), channel_id=1, source_target_pairs={{1,0},{33,32},{9,1},{41,33},{3,2},{35,34},{11,3},{43,35},{65,64},{... | collective-permute-start | bytes 774152 | tf_op jit(solution)/shard_map/ppermute | solution.py:412
  27.2 7.4 %collective-permute-start.6 = (bf16[1008,128]{1,0:T(8,128)(2,1)S(1)}, bf16[1008,128]{1,0:T(8,128)(2,1)S(1)}, u32[]{:S(2)}, u32[]{:S(2)}) collective-permute-start(bf16[1008,128]{1,0:T(8,128)(2,1)S(1)} %shard_map.92.one_ref.b0), channel_id=1, source_target_pairs={{3,0},{35,32},{25,1},{57,33},{1,2},{33,34},{27,3},{59,35},{67,64},... | collective-permute-start | bytes 774152 | tf_op jit(solution)/shard_map/ppermute | solution.py:413
  35.2 12.1 %collective-permute-start.7 = (bf16[2,1008,128]{2,1,0:T(8,128)(2,1)S(1)}, bf16[2,1008,128]{2,1,0:T(8,128)(2,1)S(1)}, u32[]{:S(2)}, u32[]{:S(2)}) collective-permute-start(bf16[2,1008,128]{2,1,0:T(8,128)(2,1)S(1)} %shard_map.94), channel_id=1, source_target_pairs={{3,0},{35,32},{25,1},{57,33},{1,2},{33,34},{27,3},{59,35},{67,64},... | collective-permute-start | bytes 1548296 | tf_op jit(solution)/shard_map/ppermute | solution.py:427
  37.1 11.8 %collective-permute-start.4 = (bf16[2,1008,128]{2,1,0:T(8,128)(2,1)S(1)}, bf16[2,1008,128]{2,1,0:T(8,128)(2,1)S(1)}, u32[]{:S(2)}, u32[]{:S(2)}) collective-permute-start(bf16[2,1008,128]{2,1,0:T(8,128)(2,1)S(1)} %shard_map.93), channel_id=1, source_target_pairs={{8,0},{40,32},{2,1},{34,33},{10,2},{42,34},{0,3},{32,35},{72,64},{... | collective-permute-start | bytes 1548296 | tf_op jit(solution)/shard_map/ppermute | solution.py:427
  38.0 13.3 %collective-permute-start.11 = (bf16[2,1008,128]{2,1,0:T(8,128)(2,1)S(1)}, bf16[2,1008,128]{2,1,0:T(8,128)(2,1)S(1)}, u32[]{:S(2)}, u32[]{:S(2)}) collective-permute-start(bf16[2,1008,128]{2,1,0:T(8,128)(2,1)S(1)} %shard_map.94), channel_id=1, source_target_pairs={{1,0},{33,32},{9,1},{41,33},{3,2},{35,34},{11,3},{43,35},{65,64},{... | collective-permute-start | bytes 1548296 | tf_op jit(solution)/shard_map/ppermute | solution.py:427
  40.3 12.0 %collective-permute-start.10 = (bf16[2,1008,128]{2,1,0:T(8,128)(2,1)S(1)}, bf16[2,1008,128]{2,1,0:T(8,128)(2,1)S(1)}, u32[]{:S(2)}, u32[]{:S(2)}) collective-permute-start(bf16[2,1008,128]{2,1,0:T(8,128)(2,1)S(1)} %shard_map.93), channel_id=1, source_target_pairs={{24,0},{56,32},{0,1},{32,33},{26,2},{58,34},{2,3},{34,35},{88,64},... | collective-permute-start | bytes 1548296 | tf_op jit(solution)/shard_map/ppermute | solution.py:427
  48.9 12.6 %collective-permute-start.8 = (bf16[2,1008,128]{2,1,0:T(8,128)(2,1)S(1)}, bf16[2,1008,128]{2,1,0:T(8,128)(2,1)S(1)}, u32[]{:S(2)}, u32[]{:S(2)}) collective-permute-start(bf16[2,1008,128]{2,1,0:T(8,128)(2,1)S(1)} %collective-permute-done.4.p0), channel_id=1, source_target_pairs={{1,0},{33,32},{9,1},{41,33},{3,2},{35,34},{11,3},{43,35},{65,64},{... | collective-permute-start | bytes 1548296 | tf_op jit(solution)/shard_map/ppermute | solution.py:441
  51.4 11.2 %collective-permute-start.9 = (bf16[2,1008,128]{2,1,0:T(8,128)(2,1)S(1)}, bf16[2,1008,128]{2,1,0:T(8,128)(2,1)S(1)}, u32[]{:S(2)}, u32[]{:S(2)}) collective-permute-start(bf16[2,1008,128]{2,1,0:T(8,128)(2,1)S(1)} %collective-permute-done.7.p3), channel_id=1, source_target_pairs={{24,0},{56,32},{0,1},{32,33},{26,2},{58,34},{2,3},{34,35},{88,64},... | collective-permute-start | bytes 1548296 | tf_op jit(solution)/shard_map/ppermute | solution.py:441
  65.3 8.6 %collective-permute-start.13 = (bf16[128,2048]{1,0:T(8,128)(2,1)S(1)}, bf16[128,2048]{1,0:T(8,128)(2,1)S(1)}, u32[]{:S(2)}, u32[]{:S(2)}) collective-permute-start(bf16[128,2048]{1,0:T(8,128)(2,1)S(1)} %get-tuple-element.36), channel_id=1, source_target_pairs={{0,32},{1,33},{2,34},{3,35},{4,36},{5,37},{6,38},{7,39},{8,40},{9,... | collective-permute-start | bytes 1572872 | tf_op jit(solution)/shard_map/ppermute | solution.py:466
  72.9 2.6 %collective-permute-start.12 = (bf16[128,2048]{1,0:T(8,128)(2,1)S(1)}, bf16[128,2048]{1,0:T(8,128)(2,1)S(1)}, u32[]{:S(2)}, u32[]{:S(2)}) collective-permute-start(bf16[128,2048]{1,0:T(8,128)(2,1)S(1)} %get-tuple-element.34), channel_id=1, source_target_pairs={{0,32},{1,33},{2,34},{3,35},{4,36},{5,37},{6,38},{7,39},{8,40},{9,... | collective-permute-start | bytes 1572872 | tf_op jit(solution)/shard_map/ppermute | solution.py:466
  74.0 8.0 %collective-permute-start.15 = (bf16[64,2048]{1,0:T(8,128)(2,1)S(1)}, bf16[64,2048]{1,0:T(8,128)(2,1)S(1)}, u32[]{:S(2)}, u32[]{:S(2)}) collective-permute-start(bf16[64,2048]{1,0:T(8,128)(2,1)S(1)} %get-tuple-element.37.refs_0_), channel_id=1, source_target_pairs={{0,64},{1,65},{2,66},{3,67},{4,68},{5,69},{6,70},{7,71},{8,72},{9,... | collective-permute-start | bytes 786440 | tf_op jit(solution)/shard_map/ppermute | solution.py:474
  75.5 12.1 %collective-permute-start.14 = (bf16[64,2048]{1,0:T(8,128)(2,1)S(1)}, bf16[64,2048]{1,0:T(8,128)(2,1)S(1)}, u32[]{:S(2)}, u32[]{:S(2)}) collective-permute-start(bf16[64,2048]{1,0:T(8,128)(2,1)S(1)} %get-tuple-element.39), channel_id=1, source_target_pairs={{0,64},{1,65},{2,66},{3,67},{4,68},{5,69},{6,70},{7,71},{8,72},{9,... | collective-permute-start | bytes 786440 | tf_op jit(solution)/shard_map/ppermute | solution.py:474
where the time goes:
time: 88.9 us; the launch traced here: 88.7 us
  waiting for transfers between devices  35 us (39%)
  starting transfers between devices  30.7 us (35%)
  Pallas kernels  20.4 us (23%)
  other arithmetic  1.37 us (2%)
    pallas_call x10, Pallas kernels, call(): pl.pallas_call(kernel, out_shape=out_shape, in_specs=in_specs, out_specs=...  18.7 us
    ppermute x2, waiting for transfers between devices, shards(): ends.append((rest, lax.ppermute(send, AXES, across)))  11 us
    ppermute x1, starting transfers between devices, shards(): low = lax.ppermute(last, AXES, side_pairs(-1))  7.39 us
    ppermute x2, waiting for transfers between devices, shards(): lax.ppermute(part, AXES, torus_pairs(even, odd))  7.1 us
    ppermute x2, starting transfers between devices, shards(): swapped = lax.ppermute(send, AXES, beside)  6.98 us
    ppermute x4, starting transfers between devices, shards(): lax.ppermute(pairs[which], AXES, torus_pairs(even, odd))  5.15 us
    ppermute x1, waiting for transfers between devices, shards(): low = lax.ppermute(last, AXES, side_pairs(-1))  4.19 us
    ppermute x4, waiting for transfers between devices, shards(): lax.ppermute(pairs[which], AXES, torus_pairs(even, odd))  3.59 us
  transfers between devices with their start and end apart: 16, of which 12 were waited for; matrix products, arithmetic and copies ran while one was open for 2% of the time, Pallas kernels for 14%

commit v1 on v0

v1 whole, which is shorter than its diff:
```python
import functools
import math

import jax
import jax.numpy as jnp
import numpy as np
from jax import lax
from jax.experimental import pallas as pl
from jax.experimental.pallas import tpu as pltpu
from jax.sharding import PartitionSpec as P

CH = 736
CHP = 768
ROWS = 64
COLS = 128
PIX = 1024
YR = 4
VPT = 1152
FOOT = 12
TZ = 256
PAY = CH + TZ + 16
STRIP = 128
STRIPS = PIX // STRIP
PIECES = ((0, 4), (4, 8))
AXES = ("segment", "slab")
SCALE = CH / PIX
F32 = jnp.float32
BF16 = jnp.bfloat16


def linear(x, y, z, core):
    return ((y % 2) * 2 + core) * 32 + (x % 4) * 8 + (y // 2) * 4 + z % 4


def devices():
    for x in range(4):
        for y in range(4):
            for z in range(4):
                for core in range(2):
                    yield x, y, z, core


def home(slab, batch, core):
    x, y_hi, z = slab // 8, slab // 4 % 2, slab % 4
    return linear(x, batch if y_hi == 0 else 3 - batch, z, core)


def batch_of(y):
    return y % 2 ^ y // 2


def main_pairs():
    return [
        (home(x * 8 + core * 4 + z, batch_of(y), core), linear(x, y, z, core))
        for x, y, z, core in devices()
        if core != y // 2
    ]


def side_pairs(shift):
    pairs = []
    for x, y, z, core in devices():
        slab = x * 8 + core * 4 + z + shift
        if 0 <= slab < 32:
            pairs.append((home(slab, batch_of(y), y // 2), linear(x, y, z, core)))
    return pairs


def torus_pairs(even, odd):
    pairs = []
    for x, y, z, core in devices():
        dx, dz = odd if (x + z) % 2 else even
        pairs.append((linear(x + dx, y, z + dz, core), linear(x, y, z, core)))
    return pairs


A1, B1, C1 = ((2, 0), (0, 2)), ((0, 1), (1, 0)), ((0, -1), (-1, 0))
NEAR = (
    (0, (1, 0), (0, 1)),
    (0, (-1, 0), (0, -1)),
    (1, (0, 1), (1, 0)),
    (1, (0, -1), (-1, 0)),
)
FAR = (
    (0, 0, (0, 1), (1, 0)),
    (1, 1, (0, -1), (-1, 0)),
    (2, 0, (1, 0), (0, 1)),
    (3, 1, (-1, 0), (0, -1)),
)


def block_table():
    table = np.zeros((16, 16), np.int32)
    for x in range(4):
        for z in range(4):

            def first(px, pz):
                odd = (px + pz) % 2
                out = [(px, pz)]
                for offsets in (A1, B1, C1):
                    dx, dz = offsets[odd]
                    out.append((px + dx, pz + dz))
                return out

            found = first(x, z)

            def second(px, pz, arrival):
                which, even, odd = NEAR[arrival]
                dx, dz = odd if (px + pz) % 2 else even
                source = first(px + dx, pz + dz)
                return source[:2] if which == 0 else source[2:]

            for arrival in range(4):
                found += second(x, z, arrival)
            for arrival, which, even, odd in FAR:
                dx, dz = odd if (x + z) % 2 else even
                found.append(second(x + dx, z + dz, arrival)[which])
            found = [(px % 4, pz % 4) for px, pz in found]
            assert len(set(found)) == 16
            table[x * 4 + z] = [px * 8 + pz for px, pz in found]
    return table


def ramp_matrix():
    distance = np.arange(CH)[:, None] - np.arange(CHP)[None, :]
    odd = distance % 2 != 0
    taps = np.where(odd, -4.0 / (math.pi**2 * np.where(odd, distance, 1) ** 2.0), 0.0)
    taps = np.where(distance == 0, 1.0, taps) * (np.arange(CHP) < CH)
    return jnp.asarray(taps.astype(np.float32).astype(BF16))


def packed(view):
    return jnp.concatenate([view[: CH // 2], view[CH // 2 :]], axis=1)


def unpacked(ref):
    return jnp.concatenate([ref[:, :ROWS], ref[:, ROWS:]], axis=0)


def column(line):
    return jnp.broadcast_to(line.reshape(1, CH), (8, CH)).T[:, :1]


def message_kernel(batch_ref, feet_hbm, raw_hbm, weight_hbm, own_ref, last_ref, first_ref, feet_ref, sem):
    batch = batch_ref[0]
    copies = [
        pltpu.make_async_copy(raw_hbm.at[batch], own_ref.at[pl.ds(0, CH)], sem.at[0]),
        pltpu.make_async_copy(weight_hbm.at[batch, 0], own_ref.at[pl.ds(CH, TZ)], sem.at[1]),
        pltpu.make_async_copy(feet_hbm, feet_ref, sem.at[2]),
    ]
    for copy in copies:
        copy.start()
    for copy in copies:
        copy.wait()
    row = lax.broadcasted_iota(jnp.int32, (16, COLS), 0)
    lane = lax.broadcasted_iota(jnp.int32, (16, COLS), 1)
    feet = jnp.full((16, COLS), -1.0, F32)
    for slot in range(FOOT):
        here = jnp.logical_and(row == 0, lane == slot)
        feet = jnp.where(here, feet_ref[batch, 0, slot].astype(F32), feet)
    own_ref[CH + TZ :, :] = feet.astype(BF16)
    raw = own_ref[:CH, :]
    last_ref[...] = packed(raw[:, ROWS:])
    first_ref[...] = packed(raw[:, :ROWS])


def pair_kernel(one_ref, two_ref, *refs):
    out_ref = refs[-1]
    out_ref[0] = one_ref[...]
    out_ref[1] = two_ref[...]


def pick_kernel(which, pair_ref, _, out_ref):
    out_ref[...] = pair_ref[which]


def prepare_kernel(_, channel_ref, view_ref, weight_ref, ramp_hbm, pick_ref, column_ref, ramp_ref, sem):
    copy = pltpu.make_async_copy(ramp_hbm, ramp_ref, sem)
    copy.start()
    sources = column(view_ref[...] * CHP + channel_ref[...])
    column_ref[...] = column(weight_ref[...])
    channel = lax.broadcasted_iota(jnp.int32, (CH, CHP), 1)
    for tap in range(3):
        pick = jnp.where(channel == sources - tap * CHP, 1.0, 0.0).astype(BF16)
        pick_ref[:, pl.ds(tap * CHP, CHP)] = pick
    copy.wait()


def filter_kernel(mine_ref, own_ref, other_ref, low_ref, high_ref, pick_ref, column_ref, ramp_ref, out_ref, x_ref, r_ref):
    keep = mine_ref[0] != 0
    both = jnp.where(keep, own_ref[...], other_ref[...])
    raw = both[:CH]
    low = jnp.concatenate([unpacked(low_ref), raw[:, :ROWS]], axis=1)
    high = jnp.concatenate([raw[:, ROWS:], unpacked(high_ref)], axis=1)
    for tap, part in enumerate((low, raw, high)):
        up = jnp.concatenate([part[1:], part[:1]], axis=0)
        rows = pl.ds(tap * CHP, CH)
        x_ref[rows, :COLS] = part
        x_ref[rows, COLS:] = up
        x_ref[pl.ds(tap * CHP + CH, CHP - CH), :] = jnp.zeros((CHP - CH, 2 * COLS), BF16)
    total = jnp.dot(pick_ref[...], x_ref[...], preferred_element_type=F32)
    weight = column_ref[...]
    r_ref[:CH, :] = ((1.0 - weight) * total[:, :COLS] + weight * total[:, COLS:]).astype(BF16)
    r_ref[CH:, :] = jnp.zeros((CHP - CH, COLS), BF16)
    out_ref[:CH, :] = jnp.dot(ramp_ref[...], r_ref[...], preferred_element_type=F32).astype(BF16)
    out_ref[CH:, :] = both[CH:]


def stage(base, names, tile_ref, f_ref, list_ref):
    lane = lax.broadcasted_iota(jnp.int32, (16, COLS), 1)
    row = lax.broadcasted_iota(jnp.int32, (16, COLS), 0)
    slots = []
    for block in names:
        feet = block[CH + TZ :, :].astype(F32)
        hit = jnp.logical_and(feet == tile_ref[0].astype(F32), row == 0)
        slots.append(jnp.sum(jnp.where(hit, lane + 1, 0).astype(F32)).astype(jnp.int32))
    list_ref[0] = 0
    for index, (slot, block) in enumerate(zip(slots, names)):

        @pl.when(slot > 0)
        def _():
            found = list_ref[0]
            f_ref[found] = block[: CH + TZ, :]
            list_ref[1 + 2 * found] = slot - 1
            list_ref[2 + 2 * found] = base + index
            list_ref[0] = found + 1


def weigh(f_ref, found, g_ref):
    col = lax.broadcasted_iota(jnp.int32, (TZ, COLS), 1)
    weight = f_ref[found, CH:, :]
    zero = jnp.zeros_like(weight)
    for view in range(2):
        part = jnp.where((col < ROWS) == (view == 0), weight, zero)
        g_ref[:, pl.ds(view * TZ, TZ)] = lax.dot_general(
            f_ref[found, :CH, :], part, (((1,), (1,)), ((), ())), preferred_element_type=F32
        ).astype(BF16)


def project(found, strips, list_ref, cos_ref, sin_ref, acc_ref, g_ref):
    slot, number = list_ref[1 + 2 * found], list_ref[2 + 2 * found]
    shift = (slot.astype(F32) - (FOOT - 1) / 2.0) * (PIX / (4.0 * FOOT))
    y_first = shift - (YR / 2.0 - 0.5)
    cos = [cos_ref[2 * number + view] * SCALE for view in range(2)]
    sin = [sin_ref[2 * number + view] * SCALE for view in range(2)]
    x_iota = lax.broadcasted_iota(jnp.int32, (STRIP, COLS), 0).astype(F32)
    c_iota = lax.broadcasted_iota(jnp.int32, (STRIP, COLS), 1).astype(F32)
    slope = [x_iota * cos[view] - c_iota for view in range(2)]
    reach = [
        jnp.minimum(0.0, (STRIP - 1) * cos[view]) + jnp.minimum(0.0, (YR - 1) * sin[view]) - 1.5
        for view in range(2)
    ]
    zero, one = jnp.zeros((), BF16), jnp.ones((), BF16)
    for place, strip in enumerate(strips):
        x_first = strip * STRIP - (PIX / 2.0 - 0.5)
        starts, parts = [], []
        for view in range(2):
            u = (CH - 1) / 2.0 + x_first * cos[view] + y_first * sin[view]
            low = jnp.clip(u + reach[view], 0.0, float(CH - COLS)).astype(jnp.int32)
            start = pl.multiple_of(lax.shift_left(lax.shift_right_logical(low, 4), 4), 16)
            offset = u - start.astype(F32)
            starts.append(start)
            rows = []
            for y in range(YR):
                away = jnp.abs((slope[view] + (offset + y * sin[view])).astype(BF16))
                rows.append(jnp.maximum(zero, one - away))
            parts.append(jnp.concatenate(rows, axis=0))
        mapped = jnp.concatenate(parts, axis=1)
        right = jnp.concatenate(
            [g_ref[pl.ds(starts[view], COLS), pl.ds(view * TZ, TZ)] for view in range(2)], axis=0
        )
        rows = pl.ds(place * (YR * STRIP), YR * STRIP)
        acc_ref[rows, :] += jnp.dot(mapped, right, preferred_element_type=F32)


def each_block(strips, list_ref, cos_ref, sin_ref, acc_ref, f_ref, g_ref, h_ref, done=None):
    count = list_ref[0]

    def step(found, now_ref, next_ref):
        weigh(f_ref, jnp.minimum(found + 1, count - 1), next_ref)
        project(found, strips, list_ref, cos_ref, sin_ref, acc_ref, now_ref)
        if done is not None:
            done(found, now_ref)

    @pl.when(count > 0)
    def _():
        weigh(f_ref, 0, g_ref)

    def two(pair, carry):
        step(2 * pair, g_ref, h_ref)

        @pl.when(2 * pair + 1 < count)
        def _():
            step(2 * pair + 1, h_ref, g_ref)

        return carry

    lax.fori_loop(0, (count + 1) // 2, two, 0)


def own_kernel(tile_ref, cos_ref, sin_ref, block_ref, acc_ref, g_ref, f_ref, list_ref):
    stage(0, [block_ref], tile_ref, f_ref, list_ref)
    acc_ref[...] = jnp.zeros_like(acc_ref)

    @pl.when(list_ref[0] > 0)
    def _():
        weigh(f_ref, 0, g_ref)
        project(0, range(STRIPS), list_ref, cos_ref, sin_ref, acc_ref, g_ref)


def first_kernel(tile_ref, cos_ref, sin_ref, b1, b2, b3, old_ref, acc_ref, g_ref, h_ref, f_ref, list_ref):
    stage(1, [b1, b2, b3], tile_ref, f_ref, list_ref)
    acc_ref[...] = old_ref[...]
    each_block(range(STRIPS), list_ref, cos_ref, sin_ref, acc_ref, f_ref, g_ref, h_ref)


def middle_kernel(tile_ref, cos_ref, sin_ref, p0, p1, p2, p3, old_ref, acc_ref, g_ref, h_ref, f_ref, list_ref):
    names = [pair.at[i] for pair in (p0, p1, p2, p3) for i in range(2)]
    stage(4, names, tile_ref, f_ref, list_ref)
    acc_ref[...] = old_ref[...]
    each_block(range(STRIPS), list_ref, cos_ref, sin_ref, acc_ref, f_ref, g_ref, h_ref)


def turn(core, acc_ref, send_ref, keep_ref):
    width = acc_ref.shape[0] // YR

    def one_strip(strip, carry):
        for y in range(YR):
            rows = pl.ds(pl.multiple_of(strip * (YR * STRIP) + y * STRIP, STRIP), STRIP)
            turned = acc_ref[rows, :].T
            cols = pl.ds(pl.multiple_of(strip * STRIP + y * width, STRIP), STRIP)
            keep_ref[:64, cols] = jnp.where(core == 0, turned[:64], turned[64:128])
            keep_ref[64:, cols] = jnp.where(core == 0, turned[128:192], turned[192:])
            send_ref[:64, cols] = jnp.where(core == 0, turned[64:128], turned[:64]).astype(BF16)
            send_ref[64:, cols] = jnp.where(core == 0, turned[192:], turned[128:192]).astype(BF16)
        return carry

    lax.fori_loop(0, width // STRIP, one_strip, 0)


def left_kernel(
    tile_ref, cos_ref, sin_ref, b0, b1, b2, b3, old_ref, send_ref, keep_ref, kept_ref, list_ref, acc_ref, g_ref, h_ref, f_ref
):
    stage(12, [b0, b1, b2, b3], tile_ref, f_ref, list_ref)
    acc_ref[...] = old_ref[: acc_ref.shape[0], :]

    def done(found, now_ref):
        kept_ref[found] = now_ref[...]

    each_block(range(*PIECES[0]), list_ref, cos_ref, sin_ref, acc_ref, f_ref, g_ref, h_ref, done)
    turn(tile_ref[1], acc_ref, send_ref, keep_ref)


def right_kernel(piece, tile_ref, cos_ref, sin_ref, list_ref, kept_ref, old_ref, send_ref, keep_ref, acc_ref):
    low, high = PIECES[piece]
    acc_ref[...] = old_ref[low * YR * STRIP : high * YR * STRIP, :]

    def one_block(found, carry):
        project(found, range(low, high), list_ref, cos_ref, sin_ref, acc_ref, kept_ref.at[found])
        return carry

    lax.fori_loop(0, list_ref[0], one_block, 0)
    turn(tile_ref[1], acc_ref, send_ref, keep_ref)


def half_kernel(chip_ref, keep_ref, got_ref, *refs):
    send_ref, rest_ref = refs[-2:]
    chip = chip_ref[0]
    mine = pl.ds(pl.multiple_of(chip * 64, 64), 64)
    theirs = pl.ds(pl.multiple_of((1 - chip) * 64, 64), 64)
    send_ref[...] = (keep_ref[theirs, :] + got_ref[theirs, :].astype(F32)).astype(BF16)
    rest_ref[...] = keep_ref[mine, :] + got_ref[mine, :].astype(F32)


def sum_kernel(piece, rest_ref, got_ref, *refs):
    out_ref, sum_ref, sem = refs[-3:]
    low, high = PIECES[piece]
    width = (high - low) * STRIP
    copies = []
    for y in range(YR):
        cols = pl.ds(y * width, width)
        sum_ref[:, cols] = rest_ref[:, cols] + got_ref[:, cols].astype(F32)
        place = out_ref.at[0, :, pl.ds(y * PIX + low * STRIP, width)]
        copies.append(pltpu.make_async_copy(sum_ref.at[:, cols], place, sem.at[y]))
    for copy in copies:
        copy.start()
    for copy in copies:
        copy.wait()


VMEM = pl.BlockSpec(memory_space=pltpu.VMEM)
SMEM = pl.BlockSpec(memory_space=pltpu.SMEM)
HBM = pl.BlockSpec(memory_space=pltpu.HBM)
LATER = pl.BlockSpec(memory_space=pl.ANY)


def stay(array):
    return pltpu.with_memory_space_constraint(array, pltpu.HBM)


def shape(dims, dtype):
    return jax.ShapeDtypeStruct(dims, dtype)


def cost(flops, moved):
    return pl.CostEstimate(flops=flops, bytes_accessed=moved, transcendentals=0)


LIMIT = 24 * 2**20
BLOCK_FLOPS = 2 * 4096 * 256 * 256 + 2 * CH * COLS * 512
PIXELS = YR * PIX


def shards(raw_views, tap_channel, tap_view, tap_weight, batch_view, footprint, plane_weight):
    segment = lax.axis_index("segment")
    slab = lax.axis_index("slab")
    chip, core = segment // 2, segment % 2
    x_pos, y_hi, z_pos = slab // 8, slab // 4 % 2, slab % 4
    batch = jnp.bitwise_xor(chip, y_hi)

    def call(kernel, out_shape, in_specs, *operands, scratch=(), work=(10**5, 10**6), limit=LIMIT):
        many = isinstance(out_shape, tuple)
        return pl.pallas_call(
            kernel,
            out_shape=out_shape,
            in_specs=in_specs,
            out_specs=tuple(SMEM if o.dtype == jnp.int32 else VMEM for o in out_shape) if many else VMEM,
            scratch_shapes=list(scratch),
            compiler_params=pltpu.CompilerParams(vmem_limit_bytes=limit),
            cost_estimate=cost(*work),
        )(*operands)

    own, last, first = call(
        message_kernel,
        (shape((PAY, COLS), BF16), shape((CH // 2, COLS), BF16), shape((CH // 2, COLS), BF16)),
        [SMEM, HBM, HBM, HBM],
        batch[None],
        stay(footprint),
        stay(raw_views),
        stay(plane_weight),
        scratch=[pltpu.SMEM((2, 1, FOOT), jnp.int32), pltpu.SemaphoreType.DMA((3,))],
    )
    other = lax.ppermute(own, AXES, main_pairs())
    low = lax.ppermute(last, AXES, side_pairs(-1))
    high = lax.ppermute(first, AXES, side_pairs(1))

    prepared = call(
        prepare_kernel,
        (shape((CH, 3 * CHP), BF16), shape((CH, 1), F32), shape((CH, CHP), BF16)),
        [LATER, VMEM, VMEM, VMEM, HBM],
        own,
        stay(tap_channel),
        stay(tap_view),
        stay(tap_weight),
        stay(ramp_matrix()),
        scratch=[pltpu.SemaphoreType.DMA],
        work=(10**6, 4 * 10**6),
    )
    payload = call(
        filter_kernel,
        shape((PAY, COLS), BF16),
        [SMEM] + [VMEM] * 7,
        (core == y_hi).astype(jnp.int32)[None],
        own,
        other,
        low,
        high,
        *prepared,
        scratch=[pltpu.VMEM((3 * CHP, 2 * COLS), BF16), pltpu.VMEM((CHP, COLS), BF16)],
        work=(4 * 10**9, 4 * 10**6),
    )
    payload, batch_view = lax.optimization_barrier((payload, batch_view))
    got_a = lax.ppermute(payload, AXES, torus_pairs(*A1))
    got_b = lax.ppermute(payload, AXES, torus_pairs(*B1))
    got_c = lax.ppermute(payload, AXES, torus_pairs(*C1))
    blocks = lax.dynamic_index_in_dim(jnp.asarray(block_table()), x_pos * 4 + z_pos, 0, keepdims=False)
    first_view = lax.dynamic_index_in_dim(batch_view, batch, 0, keepdims=False)
    views = jnp.arange(32, dtype=jnp.int32)
    angle = first_view + 2 * (jnp.repeat(blocks, 2) + core * 4) + views % 2
    theta = angle.astype(F32) * (2.0 * math.pi / VPT)
    cos, sin = jnp.cos(theta), jnp.sin(theta)
    tile = jnp.where(jnp.arange(2) == 0, slab, core).astype(jnp.int32)

    two = shape((2, PAY, COLS), BF16)
    accumulator = shape((PIXELS, TZ), F32)
    total = call(
        own_kernel, accumulator, [SMEM] * 3 + [VMEM],
        tile, cos, sin, payload,
        scratch=[pltpu.VMEM((CH, 2 * TZ), BF16), pltpu.VMEM((1, CH + TZ, COLS), BF16), pltpu.SMEM((3,), jnp.int32)],
        work=(BLOCK_FLOPS, 10**6),
    )
    pairs = (
        call(pair_kernel, two, [VMEM, VMEM], payload, got_a),
        call(pair_kernel, two, [VMEM, VMEM, LATER], got_b, got_c, total),
    )
    near = [lax.ppermute(pairs[which], AXES, torus_pairs(even, odd)) for which, even, odd in NEAR]

    def scratch(count, listed=True):
        weighed = [pltpu.VMEM((CH, 2 * TZ), BF16)] * (2 if count > 1 else 1)
        found = [pltpu.VMEM((count, CH + TZ, COLS), BF16)]
        return weighed + found + [pltpu.SMEM((1 + 2 * count,), jnp.int32)] * listed

    total = call(
        first_kernel, accumulator, [SMEM] * 3 + [VMEM] * 4,
        tile, cos, sin, got_a, got_b, got_c, total,
        scratch=scratch(3), work=(3 * BLOCK_FLOPS, 5 * 10**6),
    )
    far = []
    for arrival, which, even, odd in FAR:
        passed = call(
            functools.partial(pick_kernel, which), shape((PAY, COLS), BF16), [VMEM, LATER], near[arrival], total
        )
        far.append(lax.ppermute(passed, AXES, torus_pairs(even, odd)))
    total = call(
        middle_kernel, accumulator, [SMEM] * 3 + [VMEM] * 5,
        tile, cos, sin, *near, total,
        scratch=scratch(8), work=(8 * BLOCK_FLOPS, 10**7),
    )
    beside = [(s * 32 + t, (s ^ 1) * 32 + t) for s in range(4) for t in range(32)]
    across = [(s * 32 + t, (s ^ 2) * 32 + t) for s in range(4) for t in range(32)]
    ends, before = [], []
    for piece, (first_strip, last_strip) in enumerate(PIECES):
        pixels = (last_strip - first_strip) * STRIP * YR
        outputs = (shape((COLS, pixels), BF16), shape((COLS, pixels), F32))
        acc = [pltpu.VMEM((pixels, TZ), F32)]
        if piece == 0:
            send, keep, kept, slots = call(
                left_kernel,
                outputs + (shape((4, CH, 2 * TZ), BF16), shape((9,), jnp.int32)),
                [SMEM] * 3 + [VMEM] * 5,
                tile, cos, sin, *far, total,
                scratch=acc + scratch(4, False), work=(2 * BLOCK_FLOPS, 9 * 10**6),
            )
        else:
            send, keep = call(
                functools.partial(right_kernel, piece),
                outputs,
                [SMEM] * 4 + [VMEM] * 2,
                tile, cos, sin, slots, kept, total,
                scratch=acc, work=(BLOCK_FLOPS, 4 * 10**6),
            )
        swapped = lax.ppermute(send, AXES, beside)
        send, rest = call(
            half_kernel,
            (shape((64, pixels), BF16), shape((64, pixels), F32)),
            [SMEM, VMEM, VMEM] + [LATER] * len(before),
            chip[None], keep, swapped, *before,
        )
        before = [send]
        ends.append((rest, lax.ppermute(send, AXES, across)))
    image = None
    for piece, (rest, swapped) in enumerate(ends):
        held = [image] if piece else []
        image = pl.pallas_call(
            functools.partial(sum_kernel, piece),
            out_shape=shape((1, 64, PIXELS), F32),
            in_specs=[VMEM, VMEM] + [LATER] * len(held),
            out_specs=LATER,
            scratch_shapes=[pltpu.VMEM(rest.shape, F32), pltpu.SemaphoreType.DMA((YR,))],
            input_output_aliases={2: 0} if held else {},
            compiler_params=pltpu.CompilerParams(vmem_limit_bytes=LIMIT),
            cost_estimate=cost(10**5, 10**6),
        )(rest, swapped, *held)
    return image


def solution(mesh):
    return jax.shard_map(
        shards,
        mesh=mesh,
        in_specs=(
            P(None, None, "slab"),
            P(),
            P(),
            P(),
            P(),
            P(None, "slab", None),
            P(None, "slab", None, None),
        ),
        out_specs=P("slab", "segment", None),
        check_vma=False,
    )
```

time: 88.9 us -> 84.3 us (0.948)
  the two profiles are of different devices: /device:TPU:1 before, /device:TPU:4 now
where the time goes in v1:
time: 84.3 us; the launch traced here: 84.2 us
  starting transfers between devices  32.1 us (38%)
  Pallas kernels  27.6 us (33%)
  waiting for transfers between devices  21.7 us (26%)
  other arithmetic  1.44 us (2%)
  local copies, waits for them, and re-layouts  0.87 us (1%)
    pallas_call x16, Pallas kernels, call(): pl.pallas_call(kernel, out_shape=out_shape, in_specs=in_specs, out_specs=...  25.9 us
    ppermute x2, waiting for transfers between devices, shards(): ends.append((rest, lax.ppermute(send, AXES, across)))  9.94 us
    ppermute x4, starting transfers between devices, shards(): far.append(lax.ppermute(passed, AXES, torus_pairs(even, odd)))  6.87 us
    ppermute x1, starting transfers between devices, shards(): got_c = lax.ppermute(payload, AXES, torus_pairs(*C1))  5.11 us
    ppermute x1, starting transfers between devices, shards(): other = lax.ppermute(own, AXES, main_pairs())  4.93 us
    ppermute x1, waiting for transfers between devices, shards(): got_a = lax.ppermute(payload, AXES, torus_pairs(*A1))  4.46 us
    ppermute x4, starting transfers between devices, shards(): lax.ppermute(pairs[which], AXES, torus_pairs(even, odd))  4.41 us
    ppermute x1, starting transfers between devices, shards(): low = lax.ppermute(last, AXES, side_pairs(-1))  3.83 us
  transfers between devices with their start and end apart: 18, of which 8 were waited for; matrix products, arithmetic and copies ran while one was open for 3% of the time, Pallas kernels for 22%

profile of v1, /device:TPU:4, one launch (start us, length us, event | category | flops | bytes accessed | tf_op | source)
XLA Modules:
  0.0 84.2 jit_solution(14188986470538063772)
XLA Ops:
  0.0 1.1 %shard_map.91 = (bf16[1008,128]{1,0:T(8,128)(2,1)S(1)}, bf16[368,128]{1,0:T(8,128)(2,1)S(1)}, bf16[368,128]{1,0:T(8,128)(2,1)S(1)}) custom-call(s32[1]{0:T(128)} %bitcast.2.batch_ref, s32[2,1,12]{2,1,0:T(1,128)} %feet_hbm.1, bf16[2,736,128]{2,1,0:T(8,128)(2,1)} %raw_hbm.1, bf16[2,1,256,128]{3,2,1,0:T(8,128)(2,1)} %weight_hbm.1), custom_call_target="tpu_custom_call" | custom-call | flops 100000 | bytes 1000000 | tf_op jit(solution)/shard_map/pallas_call | solution.py:423
  1.1 4.9 %collective-permute-start = (bf16[1008,128]{1,0:T(8,128)(2,1)S(1)}, bf16[1008,128]{1,0:T(8,128)(2,1)S(1)}, u32[]{:S(2)}, u32[]{:S(2)}) collective-permute-start(bf16[1008,128]{1,0:T(8,128)(2,1)S(1)} %get-tuple-element.23._.own_ref), channel_id=1, source_target_pairs={{100,32},{101,33},{102,34},{103,35},{36,96},{37,97},{38,98},{39,99... | collective-permute-start | bytes 774152 | tf_op jit(solution)/shard_map/ppermute | solution.py:443
  6.0 3.8 %collective-permute-start.1 = (bf16[368,128]{1,0:T(8,128)(2,1)S(1)}, bf16[368,128]{1,0:T(8,128)(2,1)S(1)}, u32[]{:S(2)}, u32[]{:S(2)}) collective-permute-start(bf16[368,128]{1,0:T(8,128)(2,1)S(1)} %get-tuple-element.24), channel_id=1, source_target_pairs={{3,32},{0,1},{68,33},{1,2},{69,34},{2,3},{70,35},{67,96},{64,65},{... | collective-permute-start | bytes 282632 | tf_op jit(solution)/shard_map/ppermute | solution.py:444
  9.9 1.9 %collective-permute-start.2 = (bf16[368,128]{1,0:T(8,128)(2,1)S(1)}, bf16[368,128]{1,0:T(8,128)(2,1)S(1)}, u32[]{:S(2)}, u32[]{:S(2)}) collective-permute-start(bf16[368,128]{1,0:T(8,128)(2,1)S(1)} %get-tuple-element.25), channel_id=1, source_target_pairs={{1,0},{69,32},{2,1},{70,33},{3,2},{71,34},{68,3},{8,35},{65,64},{5... | collective-permute-start | bytes 282632 | tf_op jit(solution)/shard_map/ppermute | solution.py:445
  11.8 2.0 %shard_map.92 = (bf16[736,2304]{1,0:T(8,128)(2,1)S(1)}, f32[736,1]{1,0:T(8,128)S(1)}, bf16[736,768]{1,0:T(8,128)(2,1)S(1)}) custom-call(bf16[1008,128]{1,0:T(8,128)(2,1)S(1)} %get-tuple-element.23._.own_ref, s32[736]{0:T(1024)} %channel_ref.1, s32[736]{0:T(1024)} %view_ref.1, f32[736]{0:T(1024)} %weight_ref.1, bf16[736,768]{1,0:T(8,128)(2,1)} %constant.91.clone.ramp_hbm), custom_call_target="tpu_custom_call" | custom-call | flops 1000000 | bytes 4000000 | tf_op jit(solution)/shard_map/pallas_call | solution.py:423
  13.8 2.9 %collective-permute-done.1.low_ref = bf16[368,128]{1,0:T(8,128)(2,1)S(1)} collective-permute-done((bf16[368,128]{1,0:T(8,128)(2,1)S(1)}, bf16[368,128]{1,0:T(8,128)(2,1)S(1)}, u32[]{:S(2)}, u32[]{:S(2)}) %collective-permute-start.1) | collective-permute-done | bytes 94240 | tf_op jit(solution)/shard_map/ppermute | solution.py:444
  16.7 0.6 collective-permute-done.2.high_ref
  17.3 2.0 %shard_map.93.one_ref.block_ref = bf16[1008,128]{1,0:T(8,128)(2,1)S(1)} custom-call(s32[1]{0:T(128)} %bitcast.1.mine_ref, bf16[1008,128]{1,0:T(8,128)(2,1)S(1)} %get-tuple-element.23._.own_ref, bf16[1008,128]{1,0:T(8,128)(2,1)S(1)} %collective-permute-done.other_ref, bf16[368,128]{1,0:T(8,128)(2,1)S(1)} %collective-permute-done.1.low_ref, ...), custom_call_target="tpu_custom_call" | custom-call | flops 4000000000 | bytes 4000000 | tf_op jit(solution)/shard_map/pallas_call | solution.py:423
  19.4 0.6 collective-permute-start.5
  20.0 5.1 %collective-permute-start.6 = (bf16[1008,128]{1,0:T(8,128)(2,1)S(1)}, bf16[1008,128]{1,0:T(8,128)(2,1)S(1)}, u32[]{:S(2)}, u32[]{:S(2)}) collective-permute-start(bf16[1008,128]{1,0:T(8,128)(2,1)S(1)} %shard_map.93.one_ref.block_ref), channel_id=1, source_target_pairs={{3,0},{35,32},{25,1},{57,33},{1,2},{33,34},{27,3},{59,35},{67,64},... | collective-permute-start | bytes 774152 | tf_op jit(solution)/shard_map/ppermute | solution.py:475
  25.1 0.8 collective-permute-start.3
  25.9 0.7 dynamic_slice.8
  26.5 1.4 %add_bitcast_fusion = s32[16]{0:T(128)S(1)} fusion(s32[16,16]{1,0:T(8,128)} %constant.92.clone, s32[]{:T(128)S(6)} %select_n.51, s32[]{:T(128)S(6)} %mul.24, s32[]{:T(128)} %bitcast.3), kind=kLoop, calls=%fused_computation.4 | loop fusion | flops 48 | bytes 140 | tf_op jit(solution)/shard_map/add | solution.py:479
  28.2 1.0 %shard_map.95.old_ref.refs_0_ = f32[4096,256]{1,0:T(8,128)S(1)} custom-call(s32[2]{0:T(128)S(1)} %compare_select_fusion.tile_ref, f32[32]{0:T(128)S(1)} %cos.3.cos_ref, f32[32]{0:T(128)S(1)} %get-tuple-element.41.sin_ref, bf16[1008,128]{1,0:T(8,128)(2,1)S(1)} %shard_map.93.one_ref.block_ref), custom_call_target="tpu_custom_call" | custom-call | flops 633339904 | bytes 1000000 | tf_op jit(solution)/shard_map/pallas_call | solution.py:423
  29.4 2.6 %collective-permute-start.12 = (bf16[2,1008,128]{2,1,0:T(8,128)(2,1)S(1)}, bf16[2,1008,128]{2,1,0:T(8,128)(2,1)S(1)}, u32[]{:S(2)}, u32[]{:S(2)}) collective-permute-start(bf16[2,1008,128]{2,1,0:T(8,128)(2,1)S(1)} %shard_map.99), channel_id=1, source_target_pairs={{3,0},{35,32},{25,1},{57,33},{1,2},{33,34},{27,3},{59,35},{67,64},... | collective-permute-start | bytes 1548296 | tf_op jit(solution)/shard_map/ppermute | solution.py:496
  32.0 1.7 %collective-permute-start.10 = (bf16[2,1008,128]{2,1,0:T(8,128)(2,1)S(1)}, bf16[2,1008,128]{2,1,0:T(8,128)(2,1)S(1)}, u32[]{:S(2)}, u32[]{:S(2)}) collective-permute-start(bf16[2,1008,128]{2,1,0:T(8,128)(2,1)S(1)} %shard_map.99), channel_id=1, source_target_pairs={{1,0},{33,32},{9,1},{41,33},{3,2},{35,34},{11,3},{43,35},{65,64},{... | collective-permute-start | bytes 1548296 | tf_op jit(solution)/shard_map/ppermute | solution.py:496
  33.7 4.5 %collective-permute-done.3.two_ref.b1 = bf16[1008,128]{1,0:T(8,128)(2,1)S(1)} collective-permute-done((bf16[1008,128]{1,0:T(8,128)(2,1)S(1)}, bf16[1008,128]{1,0:T(8,128)(2,1)S(1)}, u32[]{:S(2)}, u32[]{:S(2)}) %collective-permute-start.3) | collective-permute-done | bytes 258080 | tf_op jit(solution)/shard_map/ppermute | solution.py:473
  38.3 3.3 %shard_map.96._.old_ref = f32[4096,256]{1,0:T(8,128)S(1)} custom-call(s32[2]{0:T(128)S(1)} %compare_select_fusion.tile_ref, f32[32]{0:T(128)S(1)} %cos.3.cos_ref, f32[32]{0:T(128)S(1)} %get-tuple-element.41.sin_ref, bf16[1008,128]{1,0:T(8,128)(2,1)S(1)} %collective-permute-done.3.two_ref.b1, bf16[1008,128]{1,0:T(8,128)(2,1)S(1)} %collective-permute-done.5.b2.one_ref, ...), custom_call_target="tpu_custom_call" | custom-call | flops 1900019712 | bytes 5000000 | tf_op jit(solution)/shard_map/pallas_call | solution.py:423
  41.7 1.1 %collective-permute-done.12.pair_ref.p3 = bf16[2,1008,128]{2,1,0:T(8,128)(2,1)S(1)} collective-permute-done((bf16[2,1008,128]{2,1,0:T(8,128)(2,1)S(1)}, bf16[2,1008,128]{2,1,0:T(8,128)(2,1)S(1)}, u32[]{:S(2)}, u32[]{:S(2)}) %collective-permute-start.12) | collective-permute-done | bytes 516128 | tf_op jit(solution)/shard_map/ppermute | solution.py:496
  42.8 1.3 %collective-permute-start.13 = (bf16[1008,128]{1,0:T(8,128)(2,1)S(1)}, bf16[1008,128]{1,0:T(8,128)(2,1)S(1)}, u32[]{:S(2)}, u32[]{:S(2)}) collective-permute-start(bf16[1008,128]{1,0:T(8,128)(2,1)S(1)} %shard_map.101), channel_id=1, source_target_pairs={{24,0},{56,32},{0,1},{32,33},{26,2},{58,34},{2,3},{34,35},{88,64},... | collective-permute-start | bytes 774152 | tf_op jit(solution)/shard_map/ppermute | solution.py:513
  44.1 3.5 %collective-permute-start.11 = (bf16[1008,128]{1,0:T(8,128)(2,1)S(1)}, bf16[1008,128]{1,0:T(8,128)(2,1)S(1)}, u32[]{:S(2)}, u32[]{:S(2)}) collective-permute-start(bf16[1008,128]{1,0:T(8,128)(2,1)S(1)} %shard_map.100), channel_id=1, source_target_pairs={{8,0},{40,32},{2,1},{34,33},{10,2},{42,34},{0,3},{32,35},{72,64},{... | collective-permute-start | bytes 774152 | tf_op jit(solution)/shard_map/ppermute | solution.py:513
  47.6 2.5 %collective-permute-done.8.pair_ref.p1 = bf16[2,1008,128]{2,1,0:T(8,128)(2,1)S(1)} collective-permute-done((bf16[2,1008,128]{2,1,0:T(8,128)(2,1)S(1)}, bf16[2,1008,128]{2,1,0:T(8,128)(2,1)S(1)}, u32[]{:S(2)}, u32[]{:S(2)}) %collective-permute-start.8) | collective-permute-done | bytes 516128 | tf_op jit(solution)/shard_map/ppermute | solution.py:496
  50.1 2.0 %collective-permute-start.9 = (bf16[1008,128]{1,0:T(8,128)(2,1)S(1)}, bf16[1008,128]{1,0:T(8,128)(2,1)S(1)}, u32[]{:S(2)}, u32[]{:S(2)}) collective-permute-start(bf16[1008,128]{1,0:T(8,128)(2,1)S(1)} %shard_map.98), channel_id=1, source_target_pairs={{3,0},{35,32},{25,1},{57,33},{1,2},{33,34},{27,3},{59,35},{67,64},... | collective-permute-start | bytes 774152 | tf_op jit(solution)/shard_map/ppermute | solution.py:513
  52.2 7.5 %shard_map.102.old_ref = f32[4096,256]{1,0:T(8,128)S(1)} custom-call(s32[2]{0:T(128)S(1)} %compare_select_fusion.tile_ref, f32[32]{0:T(128)S(1)} %cos.3.cos_ref, f32[32]{0:T(128)S(1)} %get-tuple-element.41.sin_ref, bf16[2,1008,128]{2,1,0:T(8,128)(2,1)S(1)} %collective-permute-done.4.pair_ref.p0, ...), custom_call_target="tpu_custom_call" | custom-call | flops 5066719232 | bytes 10000000 | tf_op jit(solution)/shard_map/pallas_call | solution.py:423
  59.7 5.3 %shard_map.103 = (bf16[128,2048]{1,0:T(8,128)(2,1)S(1)}, f32[128,2048]{1,0:T(8,128)S(1)}, bf16[4,736,512]{2,1,0:T(8,128)(2,1)S(1)}, s32[9]{0:T(128)S(1)}) custom-call(s32[2]{0:T(128)S(1)} %compare_select_fusion.tile_ref, f32[32]{0:T(128)S(1)} %cos.3.cos_ref, f32[32]{0:T(128)S(1)} %get-tuple-element.41.sin_ref, ...), custom_call_target="tpu_custom_call" | custom-call | flops 1266679808 | bytes 9000000 | tf_op jit(solution)/shard_map/pallas_call | solution.py:423
  65.1 3.4 %shard_map.104 = (bf16[128,2048]{1,0:T(8,128)(2,1)S(1)}, f32[128,2048]{1,0:T(8,128)S(1)}) custom-call(s32[2]{0:T(128)S(1)} %compare_select_fusion.tile_ref, f32[32]{0:T(128)S(1)} %cos.3.cos_ref, f32[32]{0:T(128)S(1)} %get-tuple-element.41.sin_ref, s32[9]{0:T(128)S(1)} %get-tuple-element.31.list_ref, bf16[4,736,512]{2,1,0:T(8,128)(2,1)S(1)} %get-tuple-element.32.kept_ref, ...), custom_call_target="tpu_custom_call" | custom-call | flops 633339904 | bytes 4000000 | tf_op jit(solution)/shard_map/pallas_call | solution.py:423
  69.2 1.5 %collective-permute-start.17 = (bf16[64,2048]{1,0:T(8,128)(2,1)S(1)}, bf16[64,2048]{1,0:T(8,128)(2,1)S(1)}, u32[]{:S(2)}, u32[]{:S(2)}) collective-permute-start(bf16[64,2048]{1,0:T(8,128)(2,1)S(1)} %get-tuple-element.37.refs_0_), channel_id=1, source_target_pairs={{0,64},{1,65},{2,66},{3,67},{4,68},{5,69},{6,70},{7,71},{8,72},{9,... | collective-permute-start | bytes 786440 | tf_op jit(solution)/shard_map/ppermute | solution.py:550
  70.9 1.5 %collective-permute-start.16 = (bf16[64,2048]{1,0:T(8,128)(2,1)S(1)}, bf16[64,2048]{1,0:T(8,128)(2,1)S(1)}, u32[]{:S(2)}, u32[]{:S(2)}) collective-permute-start(bf16[64,2048]{1,0:T(8,128)(2,1)S(1)} %get-tuple-element.39), channel_id=1, source_target_pairs={{0,64},{1,65},{2,66},{3,67},{4,68},{5,69},{6,70},{7,71},{8,72},{9,... | collective-permute-start | bytes 786440 | tf_op jit(solution)/shard_map/ppermute | solution.py:550
  72.3 6.1 %collective-permute-done.17.got_ref = bf16[64,2048]{1,0:T(8,128)(2,1)S(1)} collective-permute-done((bf16[64,2048]{1,0:T(8,128)(2,1)S(1)}, bf16[64,2048]{1,0:T(8,128)(2,1)S(1)}, u32[]{:S(2)}, u32[]{:S(2)}) %collective-permute-start.17) | collective-permute-done | bytes 262176 | tf_op jit(solution)/shard_map/ppermute | solution.py:550
  78.5 0.9 %shard_map.107.refs_0_ = f32[1,64,4096]{2,1,0:T(8,128)} custom-call(f32[64,2048]{1,0:T(8,128)S(1)} %get-tuple-element.40.rest_ref, bf16[64,2048]{1,0:T(8,128)(2,1)S(1)} %collective-permute-done.17.got_ref), custom_call_target="tpu_custom_call" | custom-call | flops 100000 | bytes 1000000 | tf_op jit(solution)/shard_map/pallas_call | solution.py:554
  79.3 3.8 %collective-permute-done.16.got_ref = bf16[64,2048]{1,0:T(8,128)(2,1)S(1)} collective-permute-done((bf16[64,2048]{1,0:T(8,128)(2,1)S(1)}, bf16[64,2048]{1,0:T(8,128)(2,1)S(1)}, u32[]{:S(2)}, u32[]{:S(2)}) %collective-permute-start.16) | collective-permute-done | bytes 262176 | tf_op jit(solution)/shard_map/ppermute | solution.py:550
  83.2 0.9 %shard_map.108 = f32[1,64,4096]{2,1,0:T(8,128)} custom-call(f32[64,2048]{1,0:T(8,128)S(1)} %get-tuple-element.38.rest_ref, bf16[64,2048]{1,0:T(8,128)(2,1)S(1)} %collective-permute-done.16.got_ref, f32[1,64,4096]{2,1,0:T(8,128)} %shard_map.107.refs_0_), custom_call_target="tpu_custom_call", output_to_operand_aliasing={{}: (2, {})} | custom-call | flops 100000 | bytes 1000000 | tf_op jit(solution)/shard_map/pallas_call | solution.py:554
  (31 shorter events, 1.7 us)
Async XLA Ops:
  1.1 16.3 %collective-permute-start = (bf16[1008,128]{1,0:T(8,128)(2,1)S(1)}, bf16[1008,128]{1,0:T(8,128)(2,1)S(1)}, u32[]{:S(2)}, u32[]{:S(2)}) collective-permute-start(bf16[1008,128]{1,0:T(8,128)(2,1)S(1)} %get-tuple-element.23._.own_ref), channel_id=1, source_target_pairs={{100,32},{101,33},{102,34},{103,35},{36,96},{37,97},{38,98},{39,99... | collective-permute-start | bytes 774152 | tf_op jit(solution)/shard_map/ppermute | solution.py:443
  6.0 10.7 %collective-permute-start.1 = (bf16[368,128]{1,0:T(8,128)(2,1)S(1)}, bf16[368,128]{1,0:T(8,128)(2,1)S(1)}, u32[]{:S(2)}, u32[]{:S(2)}) collective-permute-start(bf16[368,128]{1,0:T(8,128)(2,1)S(1)} %get-tuple-element.24), channel_id=1, source_target_pairs={{3,32},{0,1},{68,33},{1,2},{69,34},{2,3},{70,35},{67,96},{64,65},{... | collective-permute-start | bytes 282632 | tf_op jit(solution)/shard_map/ppermute | solution.py:444
  9.9 7.5 %collective-permute-start.2 = (bf16[368,128]{1,0:T(8,128)(2,1)S(1)}, bf16[368,128]{1,0:T(8,128)(2,1)S(1)}, u32[]{:S(2)}, u32[]{:S(2)}) collective-permute-start(bf16[368,128]{1,0:T(8,128)(2,1)S(1)} %get-tuple-element.25), channel_id=1, source_target_pairs={{1,0},{69,32},{2,1},{70,33},{3,2},{71,34},{68,3},{8,35},{65,64},{5... | collective-permute-start | bytes 282632 | tf_op jit(solution)/shard_map/ppermute | solution.py:445
  17.3 8.5 %copy-start = (s32[2]{0:T(128)S(1)}, s32[2]{0:T(128)}, u32[]{:S(2)}) copy-start(s32[2]{0:T(128)} %param.13) | copy-start | bytes 28
  19.4 9.8 %collective-permute-start.5 = (bf16[1008,128]{1,0:T(8,128)(2,1)S(1)}, bf16[1008,128]{1,0:T(8,128)(2,1)S(1)}, u32[]{:S(2)}, u32[]{:S(2)}) collective-permute-start(bf16[1008,128]{1,0:T(8,128)(2,1)S(1)} %shard_map.93.one_ref.block_ref), channel_id=1, source_target_pairs={{1,0},{33,32},{9,1},{41,33},{3,2},{35,34},{11,3},{43,35},{65,64},{... | collective-permute-start | bytes 774152 | tf_op jit(solution)/shard_map/ppermute | solution.py:474
  20.0 9.4 %collective-permute-start.6 = (bf16[1008,128]{1,0:T(8,128)(2,1)S(1)}, bf16[1008,128]{1,0:T(8,128)(2,1)S(1)}, u32[]{:S(2)}, u32[]{:S(2)}) collective-permute-start(bf16[1008,128]{1,0:T(8,128)(2,1)S(1)} %shard_map.93.one_ref.block_ref), channel_id=1, source_target_pairs={{3,0},{35,32},{25,1},{57,33},{1,2},{33,34},{27,3},{59,35},{67,64},... | collective-permute-start | bytes 774152 | tf_op jit(solution)/shard_map/ppermute | solution.py:475
  25.1 13.1 %collective-permute-start.3 = (bf16[1008,128]{1,0:T(8,128)(2,1)S(1)}, bf16[1008,128]{1,0:T(8,128)(2,1)S(1)}, u32[]{:S(2)}, u32[]{:S(2)}) collective-permute-start(bf16[1008,128]{1,0:T(8,128)(2,1)S(1)} %shard_map.93.one_ref.block_ref), channel_id=1, source_target_pairs={{16,0},{48,32},{3,1},{35,33},{18,2},{50,34},{1,3},{33,35},{80,64},... | collective-permute-start | bytes 774152 | tf_op jit(solution)/shard_map/ppermute | solution.py:473
  29.4 13.3 %collective-permute-start.12 = (bf16[2,1008,128]{2,1,0:T(8,128)(2,1)S(1)}, bf16[2,1008,128]{2,1,0:T(8,128)(2,1)S(1)}, u32[]{:S(2)}, u32[]{:S(2)}) collective-permute-start(bf16[2,1008,128]{2,1,0:T(8,128)(2,1)S(1)} %shard_map.99), channel_id=1, source_target_pairs={{3,0},{35,32},{25,1},{57,33},{1,2},{33,34},{27,3},{59,35},{67,64},... | collective-permute-start | bytes 1548296 | tf_op jit(solution)/shard_map/ppermute | solution.py:496
  32.0 12.1 %collective-permute-start.10 = (bf16[2,1008,128]{2,1,0:T(8,128)(2,1)S(1)}, bf16[2,1008,128]{2,1,0:T(8,128)(2,1)S(1)}, u32[]{:S(2)}, u32[]{:S(2)}) collective-permute-start(bf16[2,1008,128]{2,1,0:T(8,128)(2,1)S(1)} %shard_map.99), channel_id=1, source_target_pairs={{1,0},{33,32},{9,1},{41,33},{3,2},{35,34},{11,3},{43,35},{65,64},{... | collective-permute-start | bytes 1548296 | tf_op jit(solution)/shard_map/ppermute | solution.py:496
  38.2 11.9 %collective-permute-start.8 = (bf16[2,1008,128]{2,1,0:T(8,128)(2,1)S(1)}, bf16[2,1008,128]{2,1,0:T(8,128)(2,1)S(1)}, u32[]{:S(2)}, u32[]{:S(2)}) collective-permute-start(bf16[2,1008,128]{2,1,0:T(8,128)(2,1)S(1)} %shard_map.94), channel_id=1, source_target_pairs={{24,0},{56,32},{0,1},{32,33},{26,2},{58,34},{2,3},{34,35},{88,64},... | collective-permute-start | bytes 1548296 | tf_op jit(solution)/shard_map/ppermute | solution.py:496
  38.2 13.8 %collective-permute-start.4 = (bf16[2,1008,128]{2,1,0:T(8,128)(2,1)S(1)}, bf16[2,1008,128]{2,1,0:T(8,128)(2,1)S(1)}, u32[]{:S(2)}, u32[]{:S(2)}) collective-permute-start(bf16[2,1008,128]{2,1,0:T(8,128)(2,1)S(1)} %shard_map.94), channel_id=1, source_target_pairs={{8,0},{40,32},{2,1},{34,33},{10,2},{42,34},{0,3},{32,35},{72,64},{... | collective-permute-start | bytes 1548296 | tf_op jit(solution)/shard_map/ppermute | solution.py:496
  42.8 16.9 %collective-permute-start.13 = (bf16[1008,128]{1,0:T(8,128)(2,1)S(1)}, bf16[1008,128]{1,0:T(8,128)(2,1)S(1)}, u32[]{:S(2)}, u32[]{:S(2)}) collective-permute-start(bf16[1008,128]{1,0:T(8,128)(2,1)S(1)} %shard_map.101), channel_id=1, source_target_pairs={{24,0},{56,32},{0,1},{32,33},{26,2},{58,34},{2,3},{34,35},{88,64},... | collective-permute-start | bytes 774152 | tf_op jit(solution)/shard_map/ppermute | solution.py:513
  44.1 15.6 %collective-permute-start.11 = (bf16[1008,128]{1,0:T(8,128)(2,1)S(1)}, bf16[1008,128]{1,0:T(8,128)(2,1)S(1)}, u32[]{:S(2)}, u32[]{:S(2)}) collective-permute-start(bf16[1008,128]{1,0:T(8,128)(2,1)S(1)} %shard_map.100), channel_id=1, source_target_pairs={{8,0},{40,32},{2,1},{34,33},{10,2},{42,34},{0,3},{32,35},{72,64},{... | collective-permute-start | bytes 774152 | tf_op jit(solution)/shard_map/ppermute | solution.py:513
  50.1 9.6 %collective-permute-start.9 = (bf16[1008,128]{1,0:T(8,128)(2,1)S(1)}, bf16[1008,128]{1,0:T(8,128)(2,1)S(1)}, u32[]{:S(2)}, u32[]{:S(2)}) collective-permute-start(bf16[1008,128]{1,0:T(8,128)(2,1)S(1)} %shard_map.98), channel_id=1, source_target_pairs={{3,0},{35,32},{25,1},{57,33},{1,2},{33,34},{27,3},{59,35},{67,64},... | collective-permute-start | bytes 774152 | tf_op jit(solution)/shard_map/ppermute | solution.py:513
  52.1 7.6 %collective-permute-start.7 = (bf16[1008,128]{1,0:T(8,128)(2,1)S(1)}, bf16[1008,128]{1,0:T(8,128)(2,1)S(1)}, u32[]{:S(2)}, u32[]{:S(2)}) collective-permute-start(bf16[1008,128]{1,0:T(8,128)(2,1)S(1)} %shard_map.97), channel_id=1, source_target_pairs={{1,0},{33,32},{9,1},{41,33},{3,2},{35,34},{11,3},{43,35},{65,64},{... | collective-permute-start | bytes 774152 | tf_op jit(solution)/shard_map/ppermute | solution.py:513
  65.1 4.1 %collective-permute-start.15 = (bf16[128,2048]{1,0:T(8,128)(2,1)S(1)}, bf16[128,2048]{1,0:T(8,128)(2,1)S(1)}, u32[]{:S(2)}, u32[]{:S(2)}) collective-permute-start(bf16[128,2048]{1,0:T(8,128)(2,1)S(1)} %get-tuple-element.36), channel_id=1, source_target_pairs={{0,32},{1,33},{2,34},{3,35},{4,36},{5,37},{6,38},{7,39},{8,40},{9,... | collective-permute-start | bytes 1572872 | tf_op jit(solution)/shard_map/ppermute | solution.py:542
  68.5 2.2 %collective-permute-start.14 = (bf16[128,2048]{1,0:T(8,128)(2,1)S(1)}, bf16[128,2048]{1,0:T(8,128)(2,1)S(1)}, u32[]{:S(2)}, u32[]{:S(2)}) collective-permute-start(bf16[128,2048]{1,0:T(8,128)(2,1)S(1)} %get-tuple-element.34), channel_id=1, source_target_pairs={{0,32},{1,33},{2,34},{3,35},{4,36},{5,37},{6,38},{7,39},{8,40},{9,... | collective-permute-start | bytes 1572872 | tf_op jit(solution)/shard_map/ppermute | solution.py:542
  69.2 9.2 %collective-permute-start.17 = (bf16[64,2048]{1,0:T(8,128)(2,1)S(1)}, bf16[64,2048]{1,0:T(8,128)(2,1)S(1)}, u32[]{:S(2)}, u32[]{:S(2)}) collective-permute-start(bf16[64,2048]{1,0:T(8,128)(2,1)S(1)} %get-tuple-element.37.refs_0_), channel_id=1, source_target_pairs={{0,64},{1,65},{2,66},{3,67},{4,68},{5,69},{6,70},{7,71},{8,72},{9,... | collective-permute-start | bytes 786440 | tf_op jit(solution)/shard_map/ppermute | solution.py:550
  70.9 12.3 %collective-permute-start.16 = (bf16[64,2048]{1,0:T(8,128)(2,1)S(1)}, bf16[64,2048]{1,0:T(8,128)(2,1)S(1)}, u32[]{:S(2)}, u32[]{:S(2)}) collective-permute-start(bf16[64,2048]{1,0:T(8,128)(2,1)S(1)} %get-tuple-element.39), channel_id=1, source_target_pairs={{0,64},{1,65},{2,66},{3,67},{4,68},{5,69},{6,70},{7,71},{8,72},{9,... | collective-permute-start | bytes 786440 | tf_op jit(solution)/shard_map/ppermute | solution.py:550
